TPU v7x, 32 devices: a whole 2x2x4 slice. The times are simulated.
32 devices in a mesh: tm: 16 (over z, x, core), head: 2 (over y).
Axes of the slice: x: 2, y: 2, z: 4, core: 2. Of those that a mesh axis runs over, the one named last changes fastest.
Arguments:
- queries: bfloat16 [16, 392, 1024], P('tm', None, 'head'), may hold values from -6 to 6
- key_tokens: bfloat16 [16, 392, 1024], P('tm', None, 'head'), may hold values from -6 to 6
- value_tokens: bfloat16 [16, 392, 1024], P('tm', None, 'head'), may hold values from -6 to 6
- out_weight: bfloat16 [1024, 1024], P('head'), may hold values from -0.1875 to 0.1875
- out_grad: bfloat16 [16, 392, 1024], P('tm'), may hold values from -6 to 6
- clip_starts: int32 [16], P('tm'), may hold values from 0 to 1, as said below
Outputs:
- projected: bfloat16 [16, 392, 1024], P('tm', 'head')
- grad_queries: bfloat16 [16, 392, 1024], P('tm', None, 'head')
- grad_keys: bfloat16 [16, 392, 1024], P('tm', None, 'head')
- grad_values: bfloat16 [16, 392, 1024], P('tm', None, 'head')
Inputs may be any that keep to these rules, and one draw needn't show every extreme that they name: `clip_starts`: the last 8 clips never begin a new video.
All inputs are finite; a program needn't handle non-finite values.
Results may differ from a plain program's by a relative error of at most 0.0087.
Values may be sent and summed in bfloat16 or wider, within the bound.
A program may use at most 64 MiB of HBM per device.

v0:
```python
import jax
import jax.numpy as jnp
from jax import lax
from jax.sharding import PartitionSpec as P

HEAD_DIM = 64
POOL = 4
MEM = 8


def passed_along(block, axis, distance):
    devices = range(lax.axis_size(axis))
    route = [(i - distance, i) for i in devices if i - distance in devices]
    return lax.ppermute(block, axis, route)


def head_terms(query_part, key_part, value_part, column_mask, grad_part):
    scale = HEAD_DIM ** (-0.5)
    contract = (((1,), (1,)), ((), ()))
    across = (((0,), (0,)), ((), ()))
    scores = (
        lax.dot_general(query_part, key_part, contract, preferred_element_type=jnp.float32) * scale
    )
    scores = jnp.where(column_mask[None, :] > 0, scores, -1e30)
    peak = jnp.max(scores, axis=1, keepdims=True)
    expo = jnp.exp(scores - peak)
    probs = expo / jnp.sum(expo, axis=1, keepdims=True)
    weights = probs.astype(jnp.bfloat16)
    attended = jnp.dot(weights, value_part, preferred_element_type=jnp.float32).astype(jnp.bfloat16)
    grad_probs = lax.dot_general(
        grad_part, value_part, contract, preferred_element_type=jnp.float32
    )
    delta = jnp.sum(probs * grad_probs, axis=1, keepdims=True)
    grad_scores = (probs * (grad_probs - delta) * scale).astype(jnp.bfloat16)
    grad_query = jnp.dot(grad_scores, key_part, preferred_element_type=jnp.float32).astype(
        jnp.bfloat16
    )
    grad_key = lax.dot_general(grad_scores, query_part, across, preferred_element_type=jnp.float32)
    grad_value = lax.dot_general(weights, grad_part, across, preferred_element_type=jnp.float32)
    return (attended, grad_query, grad_key, grad_value)


def local(queries, key_tokens, value_tokens, out_weight, out_grad, clip_starts):
    query_rows = queries[0]
    key_rows = key_tokens[0]
    value_rows = value_tokens[0]
    token_count, local_width = query_rows.shape
    pooled_count = token_count // POOL
    local_heads = local_width // HEAD_DIM
    pooled_own = jnp.stack(
        [
            key_rows.astype(jnp.float32).reshape(pooled_count, POOL, local_width).mean(axis=1),
            value_rows.astype(jnp.float32).reshape(pooled_count, POOL, local_width).mean(axis=1),
        ]
    ).astype(jnp.bfloat16)
    keep = (1 - clip_starts[0]).astype(jnp.float32)
    slot_data = []
    slot_flags = []
    flag_pair = jnp.stack([jnp.ones((), jnp.float32), keep]).astype(jnp.bfloat16)
    running = keep
    for distance in range(1, MEM + 1):
        received, got_pair = passed_along((pooled_own, flag_pair), "tm", distance)
        slot_data.append(received)
        slot_flags.append(got_pair[0].astype(jnp.float32) * running)
        running = running * got_pair[1].astype(jnp.float32)
    memory = jnp.stack(slot_data)
    memory_keys = memory[:, 0].reshape(MEM * pooled_count, local_width)
    memory_values = memory[:, 1].reshape(MEM * pooled_count, local_width)
    key_ext = jnp.concatenate([key_rows, memory_keys], axis=0)
    value_ext = jnp.concatenate([value_rows, memory_values], axis=0)
    column_mask = jnp.concatenate(
        [jnp.ones((token_count,), jnp.float32), jnp.repeat(jnp.stack(slot_flags), pooled_count)]
    )
    grad_attended = lax.dot_general(
        out_grad[0], out_weight, (((1,), (1,)), ((), ())), preferred_element_type=jnp.float32
    ).astype(jnp.bfloat16)
    attended_parts, query_grads, key_grads, value_grads = ([], [], [], [])
    for head_number in range(local_heads):
        lower = head_number * HEAD_DIM
        upper = lower + HEAD_DIM
        outcome = head_terms(
            query_rows[:, lower:upper],
            key_ext[:, lower:upper],
            value_ext[:, lower:upper],
            column_mask,
            grad_attended[:, lower:upper],
        )
        attended_parts.append(outcome[0])
        query_grads.append(outcome[1])
        key_grads.append(outcome[2])
        value_grads.append(outcome[3])
    attended = jnp.concatenate(attended_parts, axis=1)
    grad_query_rows = jnp.concatenate(query_grads, axis=1)
    grad_key_ext = jnp.concatenate(key_grads, axis=1)
    grad_value_ext = jnp.concatenate(value_grads, axis=1)
    summed = lax.psum_scatter(
        jnp.dot(attended, out_weight, preferred_element_type=jnp.float32),
        "head",
        scatter_dimension=0,
        tiled=True,
    )
    projected = summed.astype(jnp.bfloat16)[None]
    memory_grads = jnp.stack(
        [
            grad_key_ext[token_count:].reshape(MEM, pooled_count, local_width),
            grad_value_ext[token_count:].reshape(MEM, pooled_count, local_width),
        ],
        axis=1,
    )
    returned = jnp.zeros((2, pooled_count, local_width), jnp.float32)
    for distance in range(1, MEM + 1):
        returned = returned + passed_along(
            memory_grads[distance - 1].astype(jnp.bfloat16), "tm", -distance
        ).astype(jnp.float32)
    grad_keys = (grad_key_ext[:token_count] + jnp.repeat(returned[0], POOL, axis=0) / POOL).astype(
        jnp.bfloat16
    )
    grad_values = (
        grad_value_ext[:token_count] + jnp.repeat(returned[1], POOL, axis=0) / POOL
    ).astype(jnp.bfloat16)
    return (projected, grad_query_rows[None], grad_keys[None], grad_values[None])


def solution(mesh):
    return jax.shard_map(
        local,
        mesh=mesh,
        in_specs=(
            P("tm", None, "head"),
            P("tm", None, "head"),
            P("tm", None, "head"),
            P("head", None),
            P("tm", None, None),
            P("tm"),
        ),
        out_specs=(
            P("tm", "head", None),
            P("tm", None, "head"),
            P("tm", None, "head"),
            P("tm", None, "head"),
        ),
        check_vma=False,
    )
```

profile of v0, /device:TPU:0, one launch (start us, length us, event | category | flops | bytes accessed | tf_op | source)
XLA Modules:
  0.0 260.2 jit_solution(2483815085372173388)
XLA Ops:
  1.5 6.0 %collective-permute-start.7 = (bf16[2]{0:T(256)(128)(2,1)S(1)}, bf16[2]{0:T(256)(128)(2,1)S(1)}, u32[]{:S(2)}, u32[]{:S(2)}) collective-permute-start(bf16[2]{0:T(256)(128)(2,1)S(1)} %pad_maximum_fusion.3), channel_id=1, source_target_pairs={{0,16},{2,18},{4,20},{6,22},{8,24},{10,26},{12,28},{14,30},{1,17},... | collective-permute-start | bytes 20 | tf_op jit(solution)/shard_map/ppermute | solution.py:14
  7.4 3.6 %collective-permute-start.6 = (bf16[2]{0:T(256)(128)(2,1)S(1)}, bf16[2]{0:T(256)(128)(2,1)S(1)}, u32[]{:S(2)}, u32[]{:S(2)}) collective-permute-start(bf16[2]{0:T(256)(128)(2,1)S(1)} %pad_maximum_fusion.3), channel_id=1, source_target_pairs={{0,14},{2,16},{4,18},{6,20},{8,22},{10,24},{12,26},{14,28},{16,30}... | collective-permute-start | bytes 20 | tf_op jit(solution)/shard_map/ppermute | solution.py:14
  14.4 2.6 %collective-permute-start = (bf16[2]{0:T(256)(128)(2,1)S(1)}, bf16[2]{0:T(256)(128)(2,1)S(1)}, u32[]{:S(2)}, u32[]{:S(2)}) collective-permute-start(bf16[2]{0:T(256)(128)(2,1)S(1)} %pad_maximum_fusion.3), channel_id=1, source_target_pairs={{0,2},{2,4},{4,6},{6,8},{8,10},{10,12},{12,14},{14,16},{16,18},{18... | collective-permute-start | bytes 20 | tf_op jit(solution)/shard_map/ppermute | solution.py:14
  25.1 2.8 %collective-permute-start.1 = (bf16[2]{0:T(256)(128)(2,1)S(1)}, bf16[2]{0:T(256)(128)(2,1)S(1)}, u32[]{:S(2)}, u32[]{:S(2)}) collective-permute-start(bf16[2]{0:T(256)(128)(2,1)S(1)} %pad_maximum_fusion.3), channel_id=1, source_target_pairs={{0,4},{2,6},{4,8},{6,10},{8,12},{10,14},{12,16},{14,18},{16,20},{1... | collective-permute-start | bytes 20 | tf_op jit(solution)/shard_map/ppermute | solution.py:14
  33.5 4.2 %collective-permute-start.3 = (bf16[2]{0:T(256)(128)(2,1)S(1)}, bf16[2]{0:T(256)(128)(2,1)S(1)}, u32[]{:S(2)}, u32[]{:S(2)}) collective-permute-start(bf16[2]{0:T(256)(128)(2,1)S(1)} %pad_maximum_fusion.3), channel_id=1, source_target_pairs={{0,8},{2,10},{4,12},{6,14},{8,16},{10,18},{12,20},{14,22},{16,24},... | collective-permute-start | bytes 20 | tf_op jit(solution)/shard_map/ppermute | solution.py:14
  39.6 3.5 %collective-permute-start.15 = (bf16[2,98,512]{2,1,0:T(8,128)(2,1)S(1)}, bf16[2,98,512]{2,1,0:T(8,128)(2,1)S(1)}, u32[]{:S(2)}, u32[]{:S(2)}) collective-permute-start(bf16[2,98,512]{2,1,0:T(8,128)(2,1)S(1)} %pad_maximum_fusion.2), channel_id=1, source_target_pairs={{0,16},{2,18},{4,20},{6,22},{8,24},{10,26},{12,28},{14,30},{1,17},... | collective-permute-start | bytes 602120 | tf_op jit(solution)/shard_map/ppermute | solution.py:14
  56.0 3.0 %collective-permute-start.12 = (bf16[2,98,512]{2,1,0:T(8,128)(2,1)S(1)}, bf16[2,98,512]{2,1,0:T(8,128)(2,1)S(1)}, u32[]{:S(2)}, u32[]{:S(2)}) collective-permute-start(bf16[2,98,512]{2,1,0:T(8,128)(2,1)S(1)} %pad_maximum_fusion.2), channel_id=1, source_target_pairs={{0,10},{2,12},{4,14},{6,16},{8,18},{10,20},{12,22},{14,24},{16,26}... | collective-permute-start | bytes 602120 | tf_op jit(solution)/shard_map/ppermute | solution.py:14
  59.3 3.2 %collective-permute-start.9 = (bf16[2,98,512]{2,1,0:T(8,128)(2,1)S(1)}, bf16[2,98,512]{2,1,0:T(8,128)(2,1)S(1)}, u32[]{:S(2)}, u32[]{:S(2)}) collective-permute-start(bf16[2,98,512]{2,1,0:T(8,128)(2,1)S(1)} %pad_maximum_fusion.2), channel_id=1, source_target_pairs={{0,4},{2,6},{4,8},{6,10},{8,12},{10,14},{12,16},{14,18},{16,20},{1... | collective-permute-start | bytes 602120 | tf_op jit(solution)/shard_map/ppermute | solution.py:14
  62.6 4.4 %collective-permute-done.9 = bf16[2,98,512]{2,1,0:T(8,128)(2,1)S(1)} collective-permute-done((bf16[2,98,512]{2,1,0:T(8,128)(2,1)S(1)}, bf16[2,98,512]{2,1,0:T(8,128)(2,1)S(1)}, u32[]{:S(2)}, u32[]{:S(2)}) %collective-permute-start.9) | collective-permute-done | bytes 200736 | tf_op jit(solution)/shard_map/ppermute | solution.py:14
  66.9 3.3 %collective-permute-start.10 = (bf16[2,98,512]{2,1,0:T(8,128)(2,1)S(1)}, bf16[2,98,512]{2,1,0:T(8,128)(2,1)S(1)}, u32[]{:S(2)}, u32[]{:S(2)}) collective-permute-start(bf16[2,98,512]{2,1,0:T(8,128)(2,1)S(1)} %pad_maximum_fusion.2), channel_id=1, source_target_pairs={{0,6},{2,8},{4,10},{6,12},{8,14},{10,16},{12,18},{14,20},{16,22},{... | collective-permute-start | bytes 602120 | tf_op jit(solution)/shard_map/ppermute | solution.py:14
  70.3 3.3 %collective-permute-done.10 = bf16[2,98,512]{2,1,0:T(8,128)(2,1)S(1)} collective-permute-done((bf16[2,98,512]{2,1,0:T(8,128)(2,1)S(1)}, bf16[2,98,512]{2,1,0:T(8,128)(2,1)S(1)}, u32[]{:S(2)}, u32[]{:S(2)}) %collective-permute-start.10) | collective-permute-done | bytes 200736 | tf_op jit(solution)/shard_map/ppermute | solution.py:14
  73.6 16.2 %collective-permute-start.11 = (bf16[2,98,512]{2,1,0:T(8,128)(2,1)S(1)}, bf16[2,98,512]{2,1,0:T(8,128)(2,1)S(1)}, u32[]{:S(2)}, u32[]{:S(2)}) collective-permute-start(bf16[2,98,512]{2,1,0:T(8,128)(2,1)S(1)} %pad_maximum_fusion.2), channel_id=1, source_target_pairs={{0,8},{2,10},{4,12},{6,14},{8,16},{10,18},{12,20},{14,22},{16,24},... | collective-permute-start | bytes 602120 | tf_op jit(solution)/shard_map/ppermute | solution.py:14
  89.8 2.8 %collective-permute-done.11 = bf16[2,98,512]{2,1,0:T(8,128)(2,1)S(1)} collective-permute-done((bf16[2,98,512]{2,1,0:T(8,128)(2,1)S(1)}, bf16[2,98,512]{2,1,0:T(8,128)(2,1)S(1)}, u32[]{:S(2)}, u32[]{:S(2)}) %collective-permute-start.11) | collective-permute-done | bytes 200736 | tf_op jit(solution)/shard_map/ppermute | solution.py:14
  136.0 3.2 %reshape.151 = bf16[8,1,98,512]{2,0,3,1:T(8,128)(2,1)} reshape(bf16[784,512]{0,1:T(8,128)(2,1)} %slice.308) | data formatting | bytes 1605632 | tf_op jit(solution)/shard_map/stack;reshape | solution.py:103
  139.2 2.9 %copy.263 = bf16[8,1,98,512]{3,0,2,1:T(8,128)(2,1)} copy(bf16[8,1,98,512]{2,0,3,1:T(8,128)(2,1)} %reshape.151) | data formatting | bytes 1605632 | tf_op jit(solution)/shard_map/stack;reshape | solution.py:103
  143.9 23.8 %fusion = f32[200,1024]{1,0:T(8,128)S(1)} fusion(f32[392,1024]{1,0:T(8,128)} %fusion.188), kind=kCustom, calls=%all-reduce-scatter | all-reduce-scatter fusion | flops 409601 | bytes 2425344
  170.2 2.9 %fusion.17 = bf16[392,1176]{1,0:T(8,128)(2,1)S(1)} fusion(f32[392,1176]{1,0:T(8,128)} %get-tuple-element.101, f32[392]{0:T(512)S(1)} %get-tuple-element.100, f32[392]{0:T(512)S(1)} %fusion.43, f32[1176,392]{0,1:T(8,128)} %copy-done.6, f32[392]{0:T(512)S(1)} %get-tuple-element.84), kind=kLoop, calls=%fused_computation.64 | loop fusion | flops 2765952 | bytes 4614624 | tf_op jit(solution)/shard_map/convert_element_type | solution.py:34
  181.4 2.9 %slice.307 = bf16[784,512]{0,1:T(8,128)(2,1)} slice(f32[1176,512]{0,1:T(8,128)} %convolution_dynamic-update-slice_fusion.8), slice={[392:1176], [0:512]} | slice | bytes 1605632 | tf_op jit(solution)/shard_map/slice | solution.py:105
  184.3 3.2 %reshape.150 = bf16[8,1,98,512]{2,0,3,1:T(8,128)(2,1)} reshape(bf16[784,512]{0,1:T(8,128)(2,1)} %slice.307) | data formatting | bytes 1605632 | tf_op jit(solution)/shard_map/stack;reshape | solution.py:103
  187.5 2.9 %copy.262 = bf16[8,1,98,512]{3,0,2,1:T(8,128)(2,1)} copy(bf16[8,1,98,512]{2,0,3,1:T(8,128)(2,1)} %reshape.150) | data formatting | bytes 1605632 | tf_op jit(solution)/shard_map/stack;reshape | solution.py:103
  191.9 2.7 %fusion.172 = (bf16[1,2,98,512]{3,0,2,1:T(2,128)(2,1)S(1)}, bf16[1,2,98,512]{3,0,2,1:T(2,128)(2,1)S(1)}, bf16[1,2,98,512]{3,0,2,1:T(2,128)(2,1)S(1)}, bf16[1,2,9...) fusion(bf16[8,2,98,512]{3,0,2,1:T(8,128)(2,1)S(1)} %maximum_con, ...), kind=kLoop, calls=%fused_computation.260 | loop fusion | bytes 3211264 | tf_op jit(solution)/shard_map/slice | solution.py:113
  211.4 6.1 %collective-permute-done.19 = bf16[2,98,512]{2,0,1:T(2,128)(2,1)S(1)} collective-permute-done((bf16[2,98,512]{2,0,1:T(2,128)(2,1)S(1)}, bf16[2,98,512]{2,0,1:T(2,128)(2,1)S(1)}, u32[]{:S(2)}, u32[]{:S(2)}) %collective-permute-start.19) | collective-permute-done | bytes 200736 | tf_op jit(solution)/shard_map/ppermute | solution.py:14
  226.0 2.8 %collective-permute-done.22 = bf16[2,98,512]{2,0,1:T(2,128)(2,1)} collective-permute-done((bf16[2,98,512]{2,0,1:T(2,128)(2,1)}, bf16[2,98,512]{2,0,1:T(2,128)(2,1)}, u32[]{:S(2)}, u32[]{:S(2)}) %collective-permute-start.22) | collective-permute-done | bytes 200736 | tf_op jit(solution)/shard_map/ppermute | solution.py:14
  228.7 22.6 %collective-permute-done.23 = bf16[2,98,512]{2,0,1:T(2,128)(2,1)} collective-permute-done((bf16[2,98,512]{2,0,1:T(2,128)(2,1)}, bf16[2,98,512]{2,0,1:T(2,128)(2,1)}, u32[]{:S(2)}, u32[]{:S(2)}) %collective-permute-start.23) | collective-permute-done | bytes 200736 | tf_op jit(solution)/shard_map/ppermute | solution.py:14
  (217 shorter events, 112.9 us)
Async XLA Ops:
  1.5 54.5 %collective-permute-start.7 = (bf16[2]{0:T(256)(128)(2,1)S(1)}, bf16[2]{0:T(256)(128)(2,1)S(1)}, u32[]{:S(2)}, u32[]{:S(2)}) collective-permute-start(bf16[2]{0:T(256)(128)(2,1)S(1)} %pad_maximum_fusion.3), channel_id=1, source_target_pairs={{0,16},{2,18},{4,20},{6,22},{8,24},{10,26},{12,28},{14,30},{1,17},... | collective-permute-start | bytes 20 | tf_op jit(solution)/shard_map/ppermute | solution.py:14
  7.4 44.3 %collective-permute-start.6 = (bf16[2]{0:T(256)(128)(2,1)S(1)}, bf16[2]{0:T(256)(128)(2,1)S(1)}, u32[]{:S(2)}, u32[]{:S(2)}) collective-permute-start(bf16[2]{0:T(256)(128)(2,1)S(1)} %pad_maximum_fusion.3), channel_id=1, source_target_pairs={{0,14},{2,16},{4,18},{6,20},{8,22},{10,24},{12,26},{14,28},{16,30}... | collective-permute-start | bytes 20 | tf_op jit(solution)/shard_map/ppermute | solution.py:14
  11.0 37.2 %collective-permute-start.5 = (bf16[2]{0:T(256)(128)(2,1)S(1)}, bf16[2]{0:T(256)(128)(2,1)S(1)}, u32[]{:S(2)}, u32[]{:S(2)}) collective-permute-start(bf16[2]{0:T(256)(128)(2,1)S(1)} %pad_maximum_fusion.3), channel_id=1, source_target_pairs={{0,12},{2,14},{4,16},{6,18},{8,20},{10,22},{12,24},{14,26},{16,28}... | collective-permute-start | bytes 20 | tf_op jit(solution)/shard_map/ppermute | solution.py:14
  13.1 31.8 %collective-permute-start.4 = (bf16[2]{0:T(256)(128)(2,1)S(1)}, bf16[2]{0:T(256)(128)(2,1)S(1)}, u32[]{:S(2)}, u32[]{:S(2)}) collective-permute-start(bf16[2]{0:T(256)(128)(2,1)S(1)} %pad_maximum_fusion.3), channel_id=1, source_target_pairs={{0,10},{2,12},{4,14},{6,16},{8,18},{10,20},{12,22},{14,24},{16,26}... | collective-permute-start | bytes 20 | tf_op jit(solution)/shard_map/ppermute | solution.py:14
  14.4 10.6 %collective-permute-start = (bf16[2]{0:T(256)(128)(2,1)S(1)}, bf16[2]{0:T(256)(128)(2,1)S(1)}, u32[]{:S(2)}, u32[]{:S(2)}) collective-permute-start(bf16[2]{0:T(256)(128)(2,1)S(1)} %pad_maximum_fusion.3), channel_id=1, source_target_pairs={{0,2},{2,4},{4,6},{6,8},{8,10},{10,12},{12,14},{14,16},{16,18},{18... | collective-permute-start | bytes 20 | tf_op jit(solution)/shard_map/ppermute | solution.py:14
  25.1 4.7 %collective-permute-start.1 = (bf16[2]{0:T(256)(128)(2,1)S(1)}, bf16[2]{0:T(256)(128)(2,1)S(1)}, u32[]{:S(2)}, u32[]{:S(2)}) collective-permute-start(bf16[2]{0:T(256)(128)(2,1)S(1)} %pad_maximum_fusion.3), channel_id=1, source_target_pairs={{0,4},{2,6},{4,8},{6,10},{8,12},{10,14},{12,16},{14,18},{16,20},{1... | collective-permute-start | bytes 20 | tf_op jit(solution)/shard_map/ppermute | solution.py:14
  33.5 6.1 %collective-permute-start.3 = (bf16[2]{0:T(256)(128)(2,1)S(1)}, bf16[2]{0:T(256)(128)(2,1)S(1)}, u32[]{:S(2)}, u32[]{:S(2)}) collective-permute-start(bf16[2]{0:T(256)(128)(2,1)S(1)} %pad_maximum_fusion.3), channel_id=1, source_target_pairs={{0,8},{2,10},{4,12},{6,14},{8,16},{10,18},{12,20},{14,22},{16,24},... | collective-permute-start | bytes 20 | tf_op jit(solution)/shard_map/ppermute | solution.py:14
  39.6 53.1 %collective-permute-start.15 = (bf16[2,98,512]{2,1,0:T(8,128)(2,1)S(1)}, bf16[2,98,512]{2,1,0:T(8,128)(2,1)S(1)}, u32[]{:S(2)}, u32[]{:S(2)}) collective-permute-start(bf16[2,98,512]{2,1,0:T(8,128)(2,1)S(1)} %pad_maximum_fusion.2), channel_id=1, source_target_pairs={{0,16},{2,18},{4,20},{6,22},{8,24},{10,26},{12,28},{14,30},{1,17},... | collective-permute-start | bytes 602120 | tf_op jit(solution)/shard_map/ppermute | solution.py:14
  44.9 47.7 %collective-permute-start.14 = (bf16[2,98,512]{2,1,0:T(8,128)(2,1)S(1)}, bf16[2,98,512]{2,1,0:T(8,128)(2,1)S(1)}, u32[]{:S(2)}, u32[]{:S(2)}) collective-permute-start(bf16[2,98,512]{2,1,0:T(8,128)(2,1)S(1)} %pad_maximum_fusion.2), channel_id=1, source_target_pairs={{0,14},{2,16},{4,18},{6,20},{8,22},{10,24},{12,26},{14,28},{16,30}... | collective-permute-start | bytes 602120 | tf_op jit(solution)/shard_map/ppermute | solution.py:14
  48.2 44.5 %collective-permute-start.13 = (bf16[2,98,512]{2,1,0:T(8,128)(2,1)S(1)}, bf16[2,98,512]{2,1,0:T(8,128)(2,1)S(1)}, u32[]{:S(2)}, u32[]{:S(2)}) collective-permute-start(bf16[2,98,512]{2,1,0:T(8,128)(2,1)S(1)} %pad_maximum_fusion.2), channel_id=1, source_target_pairs={{0,12},{2,14},{4,16},{6,18},{8,20},{10,22},{12,24},{14,26},{16,28}... | collective-permute-start | bytes 602120 | tf_op jit(solution)/shard_map/ppermute | solution.py:14
  51.8 7.5 %collective-permute-start.8 = (bf16[2,98,512]{2,1,0:T(8,128)(2,1)S(1)}, bf16[2,98,512]{2,1,0:T(8,128)(2,1)S(1)}, u32[]{:S(2)}, u32[]{:S(2)}) collective-permute-start(bf16[2,98,512]{2,1,0:T(8,128)(2,1)S(1)} %pad_maximum_fusion.2), channel_id=1, source_target_pairs={{0,2},{2,4},{4,6},{6,8},{8,10},{10,12},{12,14},{14,16},{16,18},{18... | collective-permute-start | bytes 602120 | tf_op jit(solution)/shard_map/ppermute | solution.py:14
  56.0 36.7 %collective-permute-start.12 = (bf16[2,98,512]{2,1,0:T(8,128)(2,1)S(1)}, bf16[2,98,512]{2,1,0:T(8,128)(2,1)S(1)}, u32[]{:S(2)}, u32[]{:S(2)}) collective-permute-start(bf16[2,98,512]{2,1,0:T(8,128)(2,1)S(1)} %pad_maximum_fusion.2), channel_id=1, source_target_pairs={{0,10},{2,12},{4,14},{6,16},{8,18},{10,20},{12,22},{14,24},{16,26}... | collective-permute-start | bytes 602120 | tf_op jit(solution)/shard_map/ppermute | solution.py:14
  59.3 7.6 %collective-permute-start.9 = (bf16[2,98,512]{2,1,0:T(8,128)(2,1)S(1)}, bf16[2,98,512]{2,1,0:T(8,128)(2,1)S(1)}, u32[]{:S(2)}, u32[]{:S(2)}) collective-permute-start(bf16[2,98,512]{2,1,0:T(8,128)(2,1)S(1)} %pad_maximum_fusion.2), channel_id=1, source_target_pairs={{0,4},{2,6},{4,8},{6,10},{8,12},{10,14},{12,16},{14,18},{16,20},{1... | collective-permute-start | bytes 602120 | tf_op jit(solution)/shard_map/ppermute | solution.py:14
  66.9 6.7 %collective-permute-start.10 = (bf16[2,98,512]{2,1,0:T(8,128)(2,1)S(1)}, bf16[2,98,512]{2,1,0:T(8,128)(2,1)S(1)}, u32[]{:S(2)}, u32[]{:S(2)}) collective-permute-start(bf16[2,98,512]{2,1,0:T(8,128)(2,1)S(1)} %pad_maximum_fusion.2), channel_id=1, source_target_pairs={{0,6},{2,8},{4,10},{6,12},{8,14},{10,16},{12,18},{14,20},{16,22},{... | collective-permute-start | bytes 602120 | tf_op jit(solution)/shard_map/ppermute | solution.py:14
  73.6 19.0 %collective-permute-start.11 = (bf16[2,98,512]{2,1,0:T(8,128)(2,1)S(1)}, bf16[2,98,512]{2,1,0:T(8,128)(2,1)S(1)}, u32[]{:S(2)}, u32[]{:S(2)}) collective-permute-start(bf16[2,98,512]{2,1,0:T(8,128)(2,1)S(1)} %pad_maximum_fusion.2), channel_id=1, source_target_pairs={{0,8},{2,10},{4,12},{6,14},{8,16},{10,18},{12,20},{14,22},{16,24},... | collective-permute-start | bytes 602120 | tf_op jit(solution)/shard_map/ppermute | solution.py:14
  167.7 37.6 %collective-permute-start.24 = (bf16[4,1024]{1,0:T(4,128)(2,1)S(1)}, bf16[4,1024]{1,0:T(4,128)(2,1)S(1)}, u32[]{:S(2)}, u32[]{:S(2)}) collective-permute-start(bf16[4,1024]{1,0:T(4,128)(2,1)S(1)} %slice.320), channel_id=1, source_target_pairs={{0,1},{2,3},{4,5},{6,7},{8,9},{10,11},{12,13},{14,15},{16,17},{18,... | collective-permute-start | bytes 24584
  195.3 13.5 %collective-permute-start.17 = (bf16[2,98,512]{2,0,1:T(2,128)(2,1)S(1)}, bf16[2,98,512]{2,0,1:T(2,128)(2,1)S(1)}, u32[]{:S(2)}, u32[]{:S(2)}) collective-permute-start(bf16[2,98,512]{2,0,1:T(2,128)(2,1)S(1)} %bitcast.260), channel_id=1, source_target_pairs={{4,0},{6,2},{8,4},{10,6},{12,8},{14,10},{16,12},{18,14},{20,16},{2... | collective-permute-start | bytes 602120 | tf_op jit(solution)/shard_map/ppermute | solution.py:14
  196.6 13.5 %collective-permute-start.18 = (bf16[2,98,512]{2,0,1:T(2,128)(2,1)S(1)}, bf16[2,98,512]{2,0,1:T(2,128)(2,1)S(1)}, u32[]{:S(2)}, u32[]{:S(2)}) collective-permute-start(bf16[2,98,512]{2,0,1:T(2,128)(2,1)S(1)} %bitcast.259), channel_id=1, source_target_pairs={{6,0},{8,2},{10,4},{12,6},{14,8},{16,10},{18,12},{20,14},{22,16},{... | collective-permute-start | bytes 602120 | tf_op jit(solution)/shard_map/ppermute | solution.py:14
  197.9 19.7 %collective-permute-start.19 = (bf16[2,98,512]{2,0,1:T(2,128)(2,1)S(1)}, bf16[2,98,512]{2,0,1:T(2,128)(2,1)S(1)}, u32[]{:S(2)}, u32[]{:S(2)}) collective-permute-start(bf16[2,98,512]{2,0,1:T(2,128)(2,1)S(1)} %bitcast.258), channel_id=1, source_target_pairs={{8,0},{10,2},{12,4},{14,6},{16,8},{18,10},{20,12},{22,14},{24,16},... | collective-permute-start | bytes 602120 | tf_op jit(solution)/shard_map/ppermute | solution.py:14
  204.0 19.7 %collective-permute-start.20 = (bf16[2,98,512]{2,0,1:T(2,128)(2,1)}, bf16[2,98,512]{2,0,1:T(2,128)(2,1)}, u32[]{:S(2)}, u32[]{:S(2)}) collective-permute-start(bf16[2,98,512]{2,0,1:T(2,128)(2,1)} %bitcast.202), channel_id=1, source_target_pairs={{10,0},{12,2},{14,4},{16,6},{18,8},{20,10},{22,12},{24,14},{26,16}... | collective-permute-start | bytes 602120 | tf_op jit(solution)/shard_map/ppermute | solution.py:14
  205.3 20.7 %collective-permute-start.21 = (bf16[2,98,512]{2,0,1:T(2,128)(2,1)}, bf16[2,98,512]{2,0,1:T(2,128)(2,1)}, u32[]{:S(2)}, u32[]{:S(2)}) collective-permute-start(bf16[2,98,512]{2,0,1:T(2,128)(2,1)} %bitcast.201), channel_id=1, source_target_pairs={{12,0},{14,2},{16,4},{18,6},{20,8},{22,10},{24,12},{26,14},{28,16}... | collective-permute-start | bytes 602120 | tf_op jit(solution)/shard_map/ppermute | solution.py:14
  208.8 19.9 %collective-permute-start.22 = (bf16[2,98,512]{2,0,1:T(2,128)(2,1)}, bf16[2,98,512]{2,0,1:T(2,128)(2,1)}, u32[]{:S(2)}, u32[]{:S(2)}) collective-permute-start(bf16[2,98,512]{2,0,1:T(2,128)(2,1)} %bitcast.200), channel_id=1, source_target_pairs={{14,0},{16,2},{18,4},{20,6},{22,8},{24,10},{26,12},{28,14},{30,16}... | collective-permute-start | bytes 602120 | tf_op jit(solution)/shard_map/ppermute | solution.py:14
  210.1 41.2 %collective-permute-start.23 = (bf16[2,98,512]{2,0,1:T(2,128)(2,1)}, bf16[2,98,512]{2,0,1:T(2,128)(2,1)}, u32[]{:S(2)}, u32[]{:S(2)}) collective-permute-start(bf16[2,98,512]{2,0,1:T(2,128)(2,1)} %bitcast.199), channel_id=1, source_target_pairs={{16,0},{18,2},{20,4},{22,6},{24,8},{26,10},{28,12},{30,14},{17,1},... | collective-permute-start | bytes 602120 | tf_op jit(solution)/shard_map/ppermute | solution.py:14
  217.5 33.8 %collective-permute-start.16 = (bf16[2,98,512]{2,0,1:T(2,128)(2,1)S(1)}, bf16[2,98,512]{2,0,1:T(2,128)(2,1)}, u32[]{:S(2)}, u32[]{:S(2)}) collective-permute-start(bf16[2,98,512]{2,0,1:T(2,128)(2,1)S(1)} %bitcast.257), channel_id=1, source_target_pairs={{2,0},{4,2},{6,4},{8,6},{10,8},{12,10},{14,12},{16,14},{18,16},{20... | collective-permute-start | bytes 602120 | tf_op jit(solution)/shard_map/ppermute | solution.py:14
  (30 other events, 305.6 us)
where the time goes:
time: 265 us; the launch traced here: 260 us
  starting transfers between devices  71.8 us (27%)
  local copies, waits for them, and re-layouts  46.5 us (18%)
  waiting for transfers between devices  46.5 us (18%)
  matrix products  39.3 us (15%)
  blocking collectives  23.8 us (9%)
  other arithmetic  19.8 us (7%)
  between operations  12.5 us (5%)
    ppermute x24, starting transfers between devices, passed_along(): return lax.ppermute(block, axis, route)  69.3 us
    ppermute x24, waiting for transfers between devices, passed_along(): return lax.ppermute(block, axis, route)  46.5 us
    unnamed x1, blocking collectives  23.8 us
    another operation x4, local copies, waits for them, and re-layouts, local(): jnp.stack([grad_key_ext[token_count:].reshape(MEM, pooled_count, local_wi...  12.2 us
    unnamed x73, local copies, waits for them, and re-layouts  10.3 us
    dot_general x8, matrix products, head_terms(): lax.dot_general(grad_part, value_part, contract, preferred_element_type=j...  9.28 us
    convert_element_type x8, other arithmetic, head_terms(): grad_scores = (probs * (grad_probs - delta) * scale).astype(jnp.bfloat16)  7.27 us
    slice x9, local copies, waits for them, and re-layouts, local(): memory_grads[distance - 1].astype(jnp.bfloat16)  7.07 us
  transfers between devices with their start and end apart: 25, of which 8 were waited for; matrix products, arithmetic and copies ran while one was open for 17% of the time, Pallas kernels for 0%

commit v1 on v0

v1 whole, which is shorter than its diff:
```python
import functools

import jax
import jax.numpy as jnp
from jax import lax
from jax.experimental import pallas as pl
from jax.experimental.pallas import tpu as pltpu
from jax.sharding import PartitionSpec as P

HEAD_DIM = 64
POOL = 4
MEM = 8
LANES = 2 * HEAD_DIM
EXCLUDED = -1e30
F32 = jnp.float32
BF16 = jnp.bfloat16
BY_COLUMN = (((1,), (1,)), ((), ()))
BY_ROW = (((0,), (0,)), ((), ()))


def attention_kernel(
    flags, q_ref, k_ref, v_ref, mem_ref, weight_ref, grad_ref,
    partial_ref, dq_ref, own_ref, memory_grad_ref,
    key_ext, value_ext, bias,
):
    step = pl.program_id(0)
    tokens = q_ref.shape[0]
    pooled = mem_ref.shape[2]
    pitch = -(-pooled // 8) * 8
    base = MEM * pitch

    @pl.when(step == 0)
    def _():
        bias[...] = jnp.full(bias.shape, EXCLUDED, F32)
        key_ext[...] = jnp.zeros(key_ext.shape, F32)
        value_ext[...] = jnp.zeros(value_ext.shape, F32)
        for slot in range(MEM):
            level = jnp.where(flags[slot] > 0, 0.0, EXCLUDED).astype(F32)
            bias[slot * pitch : slot * pitch + pooled, :] = jnp.full((pooled, LANES), level, F32)
        bias[base : base + tokens, :] = jnp.zeros((tokens, LANES), F32)

    for slot in range(MEM):
        rows = slice(slot * pitch, slot * pitch + pooled)
        key_ext[rows, :] = mem_ref[slot, 0].astype(F32)
        value_ext[rows, :] = mem_ref[slot, 1].astype(F32)
    key_ext[base : base + tokens, :] = k_ref[...].astype(F32)
    value_ext[base : base + tokens, :] = v_ref[...].astype(F32)

    scale = HEAD_DIM ** (-0.5)
    grad = lax.dot_general(grad_ref[...], weight_ref[...], BY_COLUMN, preferred_element_type=F32)
    query = q_ref[...].astype(F32)
    keys = key_ext[...]
    values = value_ext[...]
    key_pair = keys.astype(BF16)
    token_lane = lax.broadcasted_iota(jnp.int32, (tokens, LANES), 1)
    ext_lane = lax.broadcasted_iota(jnp.int32, keys.shape, 1)
    attended, dq, dk, dv = [], [], [], []
    for side in range(2):
        mine = (token_lane < HEAD_DIM) if side == 0 else (token_lane >= HEAD_DIM)
        mine_ext = (ext_lane < HEAD_DIM) if side == 0 else (ext_lane >= HEAD_DIM)
        spare = HEAD_DIM * (1 - side)
        query_aug = jnp.where(mine, query, jnp.where(token_lane == spare, 1.0, 0.0)).astype(BF16)
        key_aug = jnp.where(mine_ext, keys, bias[...]).astype(BF16)
        value_aug = jnp.where(mine_ext, values, 1.0).astype(BF16)
        scores = lax.dot_general(query_aug, key_aug, BY_COLUMN, preferred_element_type=F32)
        peak = jnp.max(scores, axis=1, keepdims=True)
        expo = jnp.exp((scores - peak) * scale)
        expo_low = expo.astype(BF16)
        gathered = jnp.dot(expo_low, value_aug, preferred_element_type=F32)
        inverse = 1.0 / pltpu.roll(gathered, HEAD_DIM, 1)
        attended_side = jnp.where(mine, gathered * inverse, 0.0)
        grad_side = jnp.where(mine, grad * inverse, 0.0).astype(BF16)
        delta = jnp.sum(grad_side.astype(F32) * attended_side, axis=1, keepdims=True)
        high = delta.astype(BF16).astype(F32)
        low = delta - high
        grad_aug = jnp.where(
            mine,
            grad_side.astype(F32),
            jnp.where(token_lane == spare, -high, jnp.where(token_lane == spare + 1, -low, 0.0)),
        ).astype(BF16)
        centred = lax.dot_general(grad_aug, value_aug, BY_COLUMN, preferred_element_type=F32)
        grad_scores = (expo * centred).astype(BF16)
        query_side = jnp.where(mine, query * scale, 0.0).astype(BF16)
        dq.append(jnp.dot(grad_scores, key_pair, preferred_element_type=F32))
        dk.append(lax.dot_general(grad_scores, query_side, BY_ROW, preferred_element_type=F32))
        dv.append(lax.dot_general(expo_low, grad_side, BY_ROW, preferred_element_type=F32))
        attended.append(attended_side)
    dq_ref[...] = (jnp.where(token_lane < HEAD_DIM, dq[0], dq[1]) * scale).astype(BF16)
    for which, total in enumerate((dk[0] + dk[1], dv[0] + dv[1])):
        for slot in range(MEM):
            memory_grad_ref[slot, which] = total[slot * pitch : slot * pitch + pooled, :].astype(BF16)
        own_ref[which] = total[base : base + tokens, :]
    share = jnp.dot(
        (attended[0] + attended[1]).astype(BF16), weight_ref[...], preferred_element_type=F32
    )

    @pl.when(step == 0)
    def _():
        partial_ref[...] = share

    @pl.when(step > 0)
    def _():
        partial_ref[...] += share


def attention(flags, queries, keys, values, memory, weight, grad):
    tokens, width = queries.shape
    full = weight.shape[1]
    pooled = memory.shape[2]
    extent = MEM * (-(-pooled // 8) * 8) + tokens
    columns = pl.BlockSpec((tokens, LANES), lambda i: (0, i))
    memory_block = pl.BlockSpec((MEM, 2, pooled, LANES), lambda i: (0, 0, 0, i))
    return pl.pallas_call(
        attention_kernel,
        grid=(width // LANES,),
        in_specs=[
            pl.BlockSpec(memory_space=pltpu.SMEM),
            columns,
            columns,
            columns,
            memory_block,
            pl.BlockSpec((LANES, full), lambda i: (i, 0)),
            pl.BlockSpec((tokens, full), lambda i: (0, 0)),
        ],
        out_specs=[
            pl.BlockSpec((tokens, full), lambda i: (0, 0)),
            columns,
            pl.BlockSpec((2, tokens, LANES), lambda i: (0, 0, i)),
            memory_block,
        ],
        out_shape=[
            jax.ShapeDtypeStruct((tokens, full), F32),
            jax.ShapeDtypeStruct((tokens, width), BF16),
            jax.ShapeDtypeStruct((2, tokens, width), F32),
            jax.ShapeDtypeStruct((MEM, 2, pooled, width), BF16),
        ],
        scratch_shapes=[pltpu.VMEM((extent, LANES), F32)] * 3,
        compiler_params=pltpu.CompilerParams(dimension_semantics=("arbitrary",)),
        name="attention",
    )(flags, queries, keys, values, memory, weight, grad)


def passed_along(block, axis, distance):
    devices = range(lax.axis_size(axis))
    route = [(i - distance, i) for i in devices if i - distance in devices]
    return lax.ppermute(block, axis, route)


def local(queries, key_tokens, value_tokens, out_weight, out_grad, clip_starts):
    token_count, local_width = queries.shape[1:]
    pooled_count = token_count // POOL
    pooled_own = (
        jnp.stack([key_tokens[0], value_tokens[0]])
        .astype(F32)
        .reshape(2, pooled_count, POOL, local_width)
        .mean(axis=2)
        .astype(BF16)
    )
    starts = lax.all_gather(clip_starts.astype(F32), "tm", tiled=True)
    mine = lax.axis_index("tm")
    running = 1 - clip_starts[0].astype(F32)
    flags = []
    for distance in range(1, MEM + 1):
        earlier = mine - distance
        flags.append(jnp.where(earlier >= 0, running, 0.0))
        running = running * (1 - starts[jnp.maximum(earlier, 0)])
    memory = jnp.stack([passed_along(pooled_own, "tm", d) for d in range(1, MEM + 1)])
    partial, dq, own, memory_grads = attention(
        jnp.stack(flags).astype(jnp.int32),
        queries[0], key_tokens[0], value_tokens[0], memory, out_weight, out_grad[0],
    )
    projected = lax.psum_scatter(partial, "head", scatter_dimension=0, tiled=True).astype(BF16)
    returned = jnp.zeros((2, pooled_count, local_width), F32)
    for distance in range(1, MEM + 1):
        returned = returned + passed_along(memory_grads[distance - 1], "tm", -distance).astype(F32)
    both = (own + jnp.repeat(returned, POOL, axis=1) / POOL).astype(BF16)
    return (projected[None], dq[None], both[:1], both[1:])


def solution(mesh):
    return jax.shard_map(
        local,
        mesh=mesh,
        in_specs=(
            P("tm", None, "head"),
            P("tm", None, "head"),
            P("tm", None, "head"),
            P("head", None),
            P("tm", None, None),
            P("tm"),
        ),
        out_specs=(
            P("tm", "head", None),
            P("tm", None, "head"),
            P("tm", None, "head"),
            P("tm", None, "head"),
        ),
        check_vma=False,
    )
```

time: 265 us -> 182 us (0.69)
  the two profiles are of different devices: /device:TPU:0 before, /device:TPU:11 now
where the time goes in v1:
time: 182 us; the launch traced here: 181 us
  blocking collectives  50.5 us (28%)
  waiting for transfers between devices  40.4 us (22%)
  starting transfers between devices  39.7 us (22%)
  Pallas kernels  28.3 us (16%)
  local copies, waits for them, and re-layouts  11.4 us (6%)
  between operations  6.87 us (4%)
  other arithmetic  4.28 us (2%)
    unnamed x2, blocking collectives  50.5 us
    ppermute x16, waiting for transfers between devices, passed_along(): return lax.ppermute(block, axis, route)  40.4 us
    ppermute x16, starting transfers between devices, passed_along(): return lax.ppermute(block, axis, route)  37.6 us
    pallas_call x1, Pallas kernels, attention(): pl.pallas_call(attention_kernel, grid=(width // LANES,), in_specs=[pl.Blo...  28.3 us
  transfers between devices with their start and end apart: 17, of which 5 were waited for; matrix products, arithmetic and copies ran while one was open for 15% of the time, Pallas kernels for 0%

profile of v1, /device:TPU:11, one launch (start us, length us, event | category | flops | bytes accessed | tf_op | source)
XLA Modules:
  0.0 181.4 jit_solution(900695962409450902)
XLA Ops:
  4.0 3.7 %collective-permute-start = (bf16[2,98,512]{2,1,0:T(8,128)(2,1)S(1)}, bf16[2,98,512]{2,1,0:T(8,128)(2,1)S(1)}, u32[]{:S(2)}, u32[]{:S(2)}) collective-permute-start(bf16[2,98,512]{2,1,0:T(8,128)(2,1)S(1)} %multiply_convert_fusion), channel_id=1, source_target_pairs={{0,2},{2,4},{4,6},{6,8},{8,10},{10,12},{12,14},{14,16},{16,18},{18... | collective-permute-start | bytes 602120 | tf_op jit(solution)/shard_map/ppermute | solution.py:146
  7.7 3.1 %collective-permute-start.1 = (bf16[2,98,512]{2,1,0:T(8,128)(2,1)S(1)}, bf16[2,98,512]{2,1,0:T(8,128)(2,1)S(1)}, u32[]{:S(2)}, u32[]{:S(2)}) collective-permute-start(bf16[2,98,512]{2,1,0:T(8,128)(2,1)S(1)} %multiply_convert_fusion), channel_id=1, source_target_pairs={{0,4},{2,6},{4,8},{6,10},{8,12},{10,14},{12,16},{14,18},{16,20},{1... | collective-permute-start | bytes 602120 | tf_op jit(solution)/shard_map/ppermute | solution.py:146
  10.8 2.3 %collective-permute-start.2 = (bf16[2,98,512]{2,1,0:T(8,128)(2,1)S(1)}, bf16[2,98,512]{2,1,0:T(8,128)(2,1)S(1)}, u32[]{:S(2)}, u32[]{:S(2)}) collective-permute-start(bf16[2,98,512]{2,1,0:T(8,128)(2,1)S(1)} %multiply_convert_fusion), channel_id=1, source_target_pairs={{0,6},{2,8},{4,10},{6,12},{8,14},{10,16},{12,18},{14,20},{16,22},{... | collective-permute-start | bytes 602120 | tf_op jit(solution)/shard_map/ppermute | solution.py:146
  13.1 2.8 %collective-permute-start.3 = (bf16[2,98,512]{2,1,0:T(8,128)(2,1)S(1)}, bf16[2,98,512]{2,1,0:T(8,128)(2,1)S(1)}, u32[]{:S(2)}, u32[]{:S(2)}) collective-permute-start(bf16[2,98,512]{2,1,0:T(8,128)(2,1)S(1)} %multiply_convert_fusion), channel_id=1, source_target_pairs={{0,8},{2,10},{4,12},{6,14},{8,16},{10,18},{12,20},{14,22},{16,24},... | collective-permute-start | bytes 602120 | tf_op jit(solution)/shard_map/ppermute | solution.py:146
  19.9 28.4 %all-reduce = f32[16]{0:T(128)S(1)} all-reduce(f32[16]{0:T(128)S(1)} %convert_dynamic-update-slice_fusion), channel_id=1, replica_groups=mesh['tm'=16,'head'=2] {'tm'}, use_global_device_ids=true, to_apply=%add | all-reduce | flops 16 | bytes 128
  54.2 1.9 %collective-permute-start.5 = (bf16[2,98,512]{2,1,0:T(8,128)(2,1)S(1)}, bf16[2,98,512]{2,1,0:T(8,128)(2,1)S(1)}, u32[]{:S(2)}, u32[]{:S(2)}) collective-permute-start(bf16[2,98,512]{2,1,0:T(8,128)(2,1)S(1)} %multiply_convert_fusion), channel_id=1, source_target_pairs={{0,12},{2,14},{4,16},{6,18},{8,20},{10,22},{12,24},{14,26},{16,28}... | collective-permute-start | bytes 602120 | tf_op jit(solution)/shard_map/ppermute | solution.py:146
  56.2 1.9 %collective-permute-start.6 = (bf16[2,98,512]{2,1,0:T(8,128)(2,1)S(1)}, bf16[2,98,512]{2,1,0:T(8,128)(2,1)S(1)}, u32[]{:S(2)}, u32[]{:S(2)}) collective-permute-start(bf16[2,98,512]{2,1,0:T(8,128)(2,1)S(1)} %multiply_convert_fusion), channel_id=1, source_target_pairs={{0,14},{2,16},{4,18},{6,20},{8,22},{10,24},{12,26},{14,28},{16,30}... | collective-permute-start | bytes 602120 | tf_op jit(solution)/shard_map/ppermute | solution.py:146
  58.1 3.5 %collective-permute-start.7 = (bf16[2,98,512]{2,1,0:T(8,128)(2,1)S(1)}, bf16[2,98,512]{2,1,0:T(8,128)(2,1)S(1)}, u32[]{:S(2)}, u32[]{:S(2)}) collective-permute-start(bf16[2,98,512]{2,1,0:T(8,128)(2,1)S(1)} %multiply_convert_fusion), channel_id=1, source_target_pairs={{0,16},{2,18},{4,20},{6,22},{8,24},{10,26},{12,28},{14,30},{1,17},... | collective-permute-start | bytes 602120 | tf_op jit(solution)/shard_map/ppermute | solution.py:146
  61.8 17.3 %collective-permute-done.6 = bf16[2,98,512]{2,1,0:T(8,128)(2,1)S(1)} collective-permute-done((bf16[2,98,512]{2,1,0:T(8,128)(2,1)S(1)}, bf16[2,98,512]{2,1,0:T(8,128)(2,1)S(1)}, u32[]{:S(2)}, u32[]{:S(2)}) %collective-permute-start.6) | collective-permute-done | bytes 200736 | tf_op jit(solution)/shard_map/ppermute | solution.py:146
  79.1 4.5 %collective-permute-done.7 = bf16[2,98,512]{2,1,0:T(8,128)(2,1)S(1)} collective-permute-done((bf16[2,98,512]{2,1,0:T(8,128)(2,1)S(1)}, bf16[2,98,512]{2,1,0:T(8,128)(2,1)S(1)}, u32[]{:S(2)}, u32[]{:S(2)}) %collective-permute-start.7) | collective-permute-done | bytes 200736 | tf_op jit(solution)/shard_map/ppermute | solution.py:146
  84.8 28.3 %attention.1 = (f32[392,1024]{1,0:T(8,128)}, bf16[392,512]{1,0:T(8,128)(2,1)}, f32[2,392,512]{2,1,0:T(8,128)}, bf16[8,2,98,512]{3,2,1,0:T(8,128)(2,1)}) custom-call(s32[8]{0:T(128)} %convert_element_type.46.flags, bf16[392,512]{1,0:T(8,128)(2,1)} %bitcast.62, bf16[392,512]{1,0:T(8,128)(2,1)} %bitcast.59, bf16[392,512]{1,0:T(8,128)(2,1)} %bitcast.60, ...), custom_call_target="tpu_custom_call" | custom-call | tf_op jit(solution)/shard_map/attention/pallas_call | solution.py:113
  113.2 2.7 %slice_bitcast_fusion.7 = (bf16[2,98,512]{2,1,0:T(8,128)(2,1)S(1)}, bf16[2,98,512]{2,1,0:T(8,128)(2,1)}, bf16[2,98,512]{2,1,0:T(8,128)(2,1)}, bf16[2,98,512]{2,1...) fusion(bf16[8,2,98,512]{3,2,1,0:T(8,128)(2,1)} %get-tuple-eleme, ...), kind=kLoop, calls=%fused_computation.21 | loop fusion | bytes 3211264 | tf_op jit(solution)/shard_map/squeeze | solution.py:175
  115.8 2.0 %collective-permute-start.10 = (bf16[2,98,512]{2,1,0:T(8,128)(2,1)}, bf16[2,98,512]{2,1,0:T(8,128)(2,1)S(1)}, u32[]{:S(2)}, u32[]{:S(2)}) collective-permute-start(bf16[2,98,512]{2,1,0:T(8,128)(2,1)} %get-tuple-element.18), channel_id=1, source_target_pairs={{6,0},{8,2},{10,4},{12,6},{14,8},{16,10},{18,12},{20,14},{22,16},{... | collective-permute-start | bytes 602120 | tf_op jit(solution)/shard_map/ppermute | solution.py:146
  117.9 1.9 %collective-permute-start.11 = (bf16[2,98,512]{2,1,0:T(8,128)(2,1)}, bf16[2,98,512]{2,1,0:T(8,128)(2,1)S(1)}, u32[]{:S(2)}, u32[]{:S(2)}) collective-permute-start(bf16[2,98,512]{2,1,0:T(8,128)(2,1)} %get-tuple-element.17), channel_id=1, source_target_pairs={{8,0},{10,2},{12,4},{14,6},{16,8},{18,10},{20,12},{22,14},{24,16},... | collective-permute-start | bytes 602120 | tf_op jit(solution)/shard_map/ppermute | solution.py:146
  119.8 1.9 %collective-permute-start.12 = (bf16[2,98,512]{2,1,0:T(8,128)(2,1)}, bf16[2,98,512]{2,1,0:T(8,128)(2,1)S(1)}, u32[]{:S(2)}, u32[]{:S(2)}) collective-permute-start(bf16[2,98,512]{2,1,0:T(8,128)(2,1)} %get-tuple-element.16), channel_id=1, source_target_pairs={{10,0},{12,2},{14,4},{16,6},{18,8},{20,10},{22,12},{24,14},{26,16}... | collective-permute-start | bytes 602120 | tf_op jit(solution)/shard_map/ppermute | solution.py:146
  121.7 22.0 %fusion = f32[200,1024]{1,0:T(8,128)S(1)} fusion(f32[392,1024]{1,0:T(8,128)S(1)} %copy-done.1), kind=kCustom, calls=%all-reduce-scatter | all-reduce-scatter fusion | flops 409601 | bytes 2425344
  143.8 2.1 %collective-permute-start.16 = (bf16[4,1024]{1,0:T(4,128)(2,1)S(1)}, bf16[4,1024]{1,0:T(4,128)(2,1)S(1)}, u32[]{:S(2)}, u32[]{:S(2)}) collective-permute-start(bf16[4,1024]{1,0:T(4,128)(2,1)S(1)} %slice.42), channel_id=1, source_target_pairs={{0,1},{2,3},{4,5},{6,7},{8,9},{10,11},{12,13},{14,15},{16,17},{18,... | collective-permute-start | bytes 24584
  145.9 1.9 %collective-permute-start.13 = (bf16[2,98,512]{2,1,0:T(8,128)(2,1)}, bf16[2,98,512]{2,1,0:T(8,128)(2,1)S(1)}, u32[]{:S(2)}, u32[]{:S(2)}) collective-permute-start(bf16[2,98,512]{2,1,0:T(8,128)(2,1)} %get-tuple-element.15), channel_id=1, source_target_pairs={{12,0},{14,2},{16,4},{18,6},{20,8},{22,10},{24,12},{26,14},{28,16}... | collective-permute-start | bytes 602120 | tf_op jit(solution)/shard_map/ppermute | solution.py:146
  147.9 1.9 %collective-permute-start.14 = (bf16[2,98,512]{2,1,0:T(8,128)(2,1)}, bf16[2,98,512]{2,1,0:T(8,128)(2,1)S(1)}, u32[]{:S(2)}, u32[]{:S(2)}) collective-permute-start(bf16[2,98,512]{2,1,0:T(8,128)(2,1)} %get-tuple-element.14), channel_id=1, source_target_pairs={{14,0},{16,2},{18,4},{20,6},{22,8},{24,10},{26,12},{28,14},{30,16}... | collective-permute-start | bytes 602120 | tf_op jit(solution)/shard_map/ppermute | solution.py:146
  151.1 3.5 %collective-permute-start.8 = (bf16[2,98,512]{2,1,0:T(8,128)(2,1)S(1)}, bf16[2,98,512]{2,1,0:T(8,128)(2,1)S(1)}, u32[]{:S(2)}, u32[]{:S(2)}) collective-permute-start(bf16[2,98,512]{2,1,0:T(8,128)(2,1)S(1)} %get-tuple-element.12), channel_id=1, source_target_pairs={{2,0},{4,2},{6,4},{8,6},{10,8},{12,10},{14,12},{16,14},{18,16},{20... | collective-permute-start | bytes 602120 | tf_op jit(solution)/shard_map/ppermute | solution.py:146
  154.6 1.9 %collective-permute-start.9 = (bf16[2,98,512]{2,1,0:T(8,128)(2,1)S(1)}, bf16[2,98,512]{2,1,0:T(8,128)(2,1)S(1)}, u32[]{:S(2)}, u32[]{:S(2)}) collective-permute-start(bf16[2,98,512]{2,1,0:T(8,128)(2,1)S(1)} %get-tuple-element.19), channel_id=1, source_target_pairs={{4,0},{6,2},{8,4},{10,6},{12,8},{14,10},{16,12},{18,14},{20,16},{2... | collective-permute-start | bytes 602120 | tf_op jit(solution)/shard_map/ppermute | solution.py:146
  159.2 3.9 %collective-permute-done.14 = bf16[2,98,512]{2,1,0:T(8,128)(2,1)S(1)} collective-permute-done((bf16[2,98,512]{2,1,0:T(8,128)(2,1)}, bf16[2,98,512]{2,1,0:T(8,128)(2,1)S(1)}, u32[]{:S(2)}, u32[]{:S(2)}) %collective-permute-start.14) | collective-permute-done | bytes 200736 | tf_op jit(solution)/shard_map/ppermute | solution.py:146
  163.2 8.0 %collective-permute-done.8 = bf16[2,98,512]{2,1,0:T(8,128)(2,1)S(1)} collective-permute-done((bf16[2,98,512]{2,1,0:T(8,128)(2,1)S(1)}, bf16[2,98,512]{2,1,0:T(8,128)(2,1)S(1)}, u32[]{:S(2)}, u32[]{:S(2)}) %collective-permute-start.8) | collective-permute-done | bytes 200736 | tf_op jit(solution)/shard_map/ppermute | solution.py:146
  171.1 6.6 %collective-permute-done.9 = bf16[2,98,512]{2,1,0:T(8,128)(2,1)S(1)} collective-permute-done((bf16[2,98,512]{2,1,0:T(8,128)(2,1)S(1)}, bf16[2,98,512]{2,1,0:T(8,128)(2,1)S(1)}, u32[]{:S(2)}, u32[]{:S(2)}) %collective-permute-start.9) | collective-permute-done | bytes 200736 | tf_op jit(solution)/shard_map/ppermute | solution.py:146
  (49 shorter events, 16.2 us)
Async XLA Ops:
  0.6 16.0 %copy-start.3 = (u32[32]{0:T(128)S(1)}, u32[32]{0:T(128)}, u32[]{:S(2)}) copy-start(u32[32]{0:T(128)} %constant.64) | copy-start | bytes 388
  4.0 50.2 %collective-permute-start = (bf16[2,98,512]{2,1,0:T(8,128)(2,1)S(1)}, bf16[2,98,512]{2,1,0:T(8,128)(2,1)S(1)}, u32[]{:S(2)}, u32[]{:S(2)}) collective-permute-start(bf16[2,98,512]{2,1,0:T(8,128)(2,1)S(1)} %multiply_convert_fusion), channel_id=1, source_target_pairs={{0,2},{2,4},{4,6},{6,8},{8,10},{10,12},{12,14},{14,16},{16,18},{18... | collective-permute-start | bytes 602120 | tf_op jit(solution)/shard_map/ppermute | solution.py:146
  7.7 48.4 %collective-permute-start.1 = (bf16[2,98,512]{2,1,0:T(8,128)(2,1)S(1)}, bf16[2,98,512]{2,1,0:T(8,128)(2,1)S(1)}, u32[]{:S(2)}, u32[]{:S(2)}) collective-permute-start(bf16[2,98,512]{2,1,0:T(8,128)(2,1)S(1)} %multiply_convert_fusion), channel_id=1, source_target_pairs={{0,4},{2,6},{4,8},{6,10},{8,12},{10,14},{12,16},{14,18},{16,20},{1... | collective-permute-start | bytes 602120 | tf_op jit(solution)/shard_map/ppermute | solution.py:146
  10.8 47.3 %collective-permute-start.2 = (bf16[2,98,512]{2,1,0:T(8,128)(2,1)S(1)}, bf16[2,98,512]{2,1,0:T(8,128)(2,1)S(1)}, u32[]{:S(2)}, u32[]{:S(2)}) collective-permute-start(bf16[2,98,512]{2,1,0:T(8,128)(2,1)S(1)} %multiply_convert_fusion), channel_id=1, source_target_pairs={{0,6},{2,8},{4,10},{6,12},{8,14},{10,16},{12,18},{14,20},{16,22},{... | collective-permute-start | bytes 602120 | tf_op jit(solution)/shard_map/ppermute | solution.py:146
  13.1 48.5 %collective-permute-start.3 = (bf16[2,98,512]{2,1,0:T(8,128)(2,1)S(1)}, bf16[2,98,512]{2,1,0:T(8,128)(2,1)S(1)}, u32[]{:S(2)}, u32[]{:S(2)}) collective-permute-start(bf16[2,98,512]{2,1,0:T(8,128)(2,1)S(1)} %multiply_convert_fusion), channel_id=1, source_target_pairs={{0,8},{2,10},{4,12},{6,14},{8,16},{10,18},{12,20},{14,22},{16,24},... | collective-permute-start | bytes 602120 | tf_op jit(solution)/shard_map/ppermute | solution.py:146
  18.0 43.7 %collective-permute-start.4 = (bf16[2,98,512]{2,1,0:T(8,128)(2,1)S(1)}, bf16[2,98,512]{2,1,0:T(8,128)(2,1)S(1)}, u32[]{:S(2)}, u32[]{:S(2)}) collective-permute-start(bf16[2,98,512]{2,1,0:T(8,128)(2,1)S(1)} %multiply_convert_fusion), channel_id=1, source_target_pairs={{0,10},{2,12},{4,14},{6,16},{8,18},{10,20},{12,22},{14,24},{16,26}... | collective-permute-start | bytes 602120 | tf_op jit(solution)/shard_map/ppermute | solution.py:146
  54.2 7.5 %collective-permute-start.5 = (bf16[2,98,512]{2,1,0:T(8,128)(2,1)S(1)}, bf16[2,98,512]{2,1,0:T(8,128)(2,1)S(1)}, u32[]{:S(2)}, u32[]{:S(2)}) collective-permute-start(bf16[2,98,512]{2,1,0:T(8,128)(2,1)S(1)} %multiply_convert_fusion), channel_id=1, source_target_pairs={{0,12},{2,14},{4,16},{6,18},{8,20},{10,22},{12,24},{14,26},{16,28}... | collective-permute-start | bytes 602120 | tf_op jit(solution)/shard_map/ppermute | solution.py:146
  56.2 22.9 %collective-permute-start.6 = (bf16[2,98,512]{2,1,0:T(8,128)(2,1)S(1)}, bf16[2,98,512]{2,1,0:T(8,128)(2,1)S(1)}, u32[]{:S(2)}, u32[]{:S(2)}) collective-permute-start(bf16[2,98,512]{2,1,0:T(8,128)(2,1)S(1)} %multiply_convert_fusion), channel_id=1, source_target_pairs={{0,14},{2,16},{4,18},{6,20},{8,22},{10,24},{12,26},{14,28},{16,30}... | collective-permute-start | bytes 602120 | tf_op jit(solution)/shard_map/ppermute | solution.py:146
  58.1 25.5 %collective-permute-start.7 = (bf16[2,98,512]{2,1,0:T(8,128)(2,1)S(1)}, bf16[2,98,512]{2,1,0:T(8,128)(2,1)S(1)}, u32[]{:S(2)}, u32[]{:S(2)}) collective-permute-start(bf16[2,98,512]{2,1,0:T(8,128)(2,1)S(1)} %multiply_convert_fusion), channel_id=1, source_target_pairs={{0,16},{2,18},{4,20},{6,22},{8,24},{10,26},{12,28},{14,30},{1,17},... | collective-permute-start | bytes 602120 | tf_op jit(solution)/shard_map/ppermute | solution.py:146
  83.7 1.2 copy-start
  113.1 8.6 %copy-start.1 = (f32[392,1024]{1,0:T(8,128)S(1)}, f32[392,1024]{1,0:T(8,128)}, u32[]{:S(2)}) copy-start(f32[392,1024]{1,0:T(8,128)} %get-tuple-element.8) | copy-start | bytes 4816900
  115.8 40.7 %copy-start.2 = (u32[32]{0:T(128)S(1)}, u32[32]{0:T(128)}, u32[]{:S(2)}) copy-start(u32[32]{0:T(128)} %constant.70) | copy-start | bytes 388
  115.8 34.0 %collective-permute-start.10 = (bf16[2,98,512]{2,1,0:T(8,128)(2,1)}, bf16[2,98,512]{2,1,0:T(8,128)(2,1)S(1)}, u32[]{:S(2)}, u32[]{:S(2)}) collective-permute-start(bf16[2,98,512]{2,1,0:T(8,128)(2,1)} %get-tuple-element.18), channel_id=1, source_target_pairs={{6,0},{8,2},{10,4},{12,6},{14,8},{16,10},{18,12},{20,14},{22,16},{... | collective-permute-start | bytes 602120 | tf_op jit(solution)/shard_map/ppermute | solution.py:146
  117.9 33.2 %collective-permute-start.11 = (bf16[2,98,512]{2,1,0:T(8,128)(2,1)}, bf16[2,98,512]{2,1,0:T(8,128)(2,1)S(1)}, u32[]{:S(2)}, u32[]{:S(2)}) collective-permute-start(bf16[2,98,512]{2,1,0:T(8,128)(2,1)} %get-tuple-element.17), channel_id=1, source_target_pairs={{8,0},{10,2},{12,4},{14,6},{16,8},{18,10},{20,12},{22,14},{24,16},... | collective-permute-start | bytes 602120 | tf_op jit(solution)/shard_map/ppermute | solution.py:146
  119.8 34.8 %collective-permute-start.12 = (bf16[2,98,512]{2,1,0:T(8,128)(2,1)}, bf16[2,98,512]{2,1,0:T(8,128)(2,1)S(1)}, u32[]{:S(2)}, u32[]{:S(2)}) collective-permute-start(bf16[2,98,512]{2,1,0:T(8,128)(2,1)} %get-tuple-element.16), channel_id=1, source_target_pairs={{10,0},{12,2},{14,4},{16,6},{18,8},{20,10},{22,12},{24,14},{26,16}... | collective-permute-start | bytes 602120 | tf_op jit(solution)/shard_map/ppermute | solution.py:146
  143.8 4.0 %collective-permute-start.16 = (bf16[4,1024]{1,0:T(4,128)(2,1)S(1)}, bf16[4,1024]{1,0:T(4,128)(2,1)S(1)}, u32[]{:S(2)}, u32[]{:S(2)}) collective-permute-start(bf16[4,1024]{1,0:T(4,128)(2,1)S(1)} %slice.42), channel_id=1, source_target_pairs={{0,1},{2,3},{4,5},{6,7},{8,9},{10,11},{12,13},{14,15},{16,17},{18,... | collective-permute-start | bytes 24584
  145.9 13.3 %collective-permute-start.13 = (bf16[2,98,512]{2,1,0:T(8,128)(2,1)}, bf16[2,98,512]{2,1,0:T(8,128)(2,1)S(1)}, u32[]{:S(2)}, u32[]{:S(2)}) collective-permute-start(bf16[2,98,512]{2,1,0:T(8,128)(2,1)} %get-tuple-element.15), channel_id=1, source_target_pairs={{12,0},{14,2},{16,4},{18,6},{20,8},{22,10},{24,12},{26,14},{28,16}... | collective-permute-start | bytes 602120 | tf_op jit(solution)/shard_map/ppermute | solution.py:146
  147.9 15.3 %collective-permute-start.14 = (bf16[2,98,512]{2,1,0:T(8,128)(2,1)}, bf16[2,98,512]{2,1,0:T(8,128)(2,1)S(1)}, u32[]{:S(2)}, u32[]{:S(2)}) collective-permute-start(bf16[2,98,512]{2,1,0:T(8,128)(2,1)} %get-tuple-element.14), channel_id=1, source_target_pairs={{14,0},{16,2},{18,4},{20,6},{22,8},{24,10},{26,12},{28,14},{30,16}... | collective-permute-start | bytes 602120 | tf_op jit(solution)/shard_map/ppermute | solution.py:146
  149.8 13.4 %collective-permute-start.15 = (bf16[2,98,512]{2,1,0:T(8,128)(2,1)}, bf16[2,98,512]{2,1,0:T(8,128)(2,1)S(1)}, u32[]{:S(2)}, u32[]{:S(2)}) collective-permute-start(bf16[2,98,512]{2,1,0:T(8,128)(2,1)} %get-tuple-element.13), channel_id=1, source_target_pairs={{16,0},{18,2},{20,4},{22,6},{24,8},{26,10},{28,12},{30,14},{17,1},... | collective-permute-start | bytes 602120 | tf_op jit(solution)/shard_map/ppermute | solution.py:146
  151.1 20.0 %collective-permute-start.8 = (bf16[2,98,512]{2,1,0:T(8,128)(2,1)S(1)}, bf16[2,98,512]{2,1,0:T(8,128)(2,1)S(1)}, u32[]{:S(2)}, u32[]{:S(2)}) collective-permute-start(bf16[2,98,512]{2,1,0:T(8,128)(2,1)S(1)} %get-tuple-element.12), channel_id=1, source_target_pairs={{2,0},{4,2},{6,4},{8,6},{10,8},{12,10},{14,12},{16,14},{18,16},{20... | collective-permute-start | bytes 602120 | tf_op jit(solution)/shard_map/ppermute | solution.py:146
  154.6 23.1 %collective-permute-start.9 = (bf16[2,98,512]{2,1,0:T(8,128)(2,1)S(1)}, bf16[2,98,512]{2,1,0:T(8,128)(2,1)S(1)}, u32[]{:S(2)}, u32[]{:S(2)}) collective-permute-start(bf16[2,98,512]{2,1,0:T(8,128)(2,1)S(1)} %get-tuple-element.19), channel_id=1, source_target_pairs={{4,0},{6,2},{8,4},{10,6},{12,8},{14,10},{16,12},{18,14},{20,16},{2... | collective-permute-start | bytes 602120 | tf_op jit(solution)/shard_map/ppermute | solution.py:146

commit v2 on v1

--- a/solution.py
+++ b/solution.py
@@ -10,6 +10,7 @@
 HEAD_DIM = 64
 POOL = 4
 MEM = 8
+GROUP = 4
 LANES = 2 * HEAD_DIM
 EXCLUDED = -1e30
 F32 = jnp.float32
@@ -19,28 +20,30 @@
 
 
 def attention_kernel(
-    flags, q_ref, k_ref, v_ref, mem_ref, weight_ref, grad_ref,
-    partial_ref, dq_ref, own_ref, memory_grad_ref,
-    key_ext, value_ext, bias,
+    start, q_ref, k_ref, v_ref, mem_ref, weight_ref, grad_ref,
+    share_ref, dq_ref, own_ref, memory_grad_ref,
+    key_ext, value_ext, bias, partial_ref,
 ):
     step = pl.program_id(0)
     tokens = q_ref.shape[0]
-    pooled = mem_ref.shape[2]
-    pitch = -(-pooled // 8) * 8
+    pooled = tokens // POOL
+    pitch = mem_ref.shape[2]
     base = MEM * pitch
 
     @pl.when(step == 0)
     def _():
         bias[...] = jnp.full(bias.shape, EXCLUDED, F32)
-        key_ext[...] = jnp.zeros(key_ext.shape, F32)
-        value_ext[...] = jnp.zeros(value_ext.shape, F32)
+        running = jnp.full((1, LANES), 1 - start[0], jnp.int32).astype(F32)
         for slot in range(MEM):
-            level = jnp.where(flags[slot] > 0, 0.0, EXCLUDED).astype(F32)
-            bias[slot * pitch : slot * pitch + pooled, :] = jnp.full((pooled, LANES), level, F32)
+            keep = mem_ref[slot, 0, pooled : pooled + 1, :].astype(F32)
+            exists = mem_ref[slot, 0, pooled + 1 : pooled + 2, :].astype(F32)
+            level = (1.0 - running * exists) * EXCLUDED
+            bias[slot * pitch : slot * pitch + pooled, :] = jnp.broadcast_to(level, (pooled, LANES))
+            running = running * keep
         bias[base : base + tokens, :] = jnp.zeros((tokens, LANES), F32)
 
     for slot in range(MEM):
-        rows = slice(slot * pitch, slot * pitch + pooled)
+        rows = slice(slot * pitch, (slot + 1) * pitch)
         key_ext[rows, :] = mem_ref[slot, 0].astype(F32)
         value_ext[rows, :] = mem_ref[slot, 1].astype(F32)
     key_ext[base : base + tokens, :] = k_ref[...].astype(F32)
@@ -88,7 +91,7 @@
     dq_ref[...] = (jnp.where(token_lane < HEAD_DIM, dq[0], dq[1]) * scale).astype(BF16)
     for which, total in enumerate((dk[0] + dk[1], dv[0] + dv[1])):
         for slot in range(MEM):
-            memory_grad_ref[slot, which] = total[slot * pitch : slot * pitch + pooled, :].astype(BF16)
+            memory_grad_ref[slot, which] = total[slot * pitch : (slot + 1) * pitch, :].astype(BF16)
         own_ref[which] = total[base : base + tokens, :]
     share = jnp.dot(
         (attended[0] + attended[1]).astype(BF16), weight_ref[...], preferred_element_type=F32
@@ -102,14 +105,20 @@
     def _():
         partial_ref[...] += share
 
-
-def attention(flags, queries, keys, values, memory, weight, grad):
+    @pl.when(step == pl.num_programs(0) - 1)
+    def _():
+        rows = share_ref.shape[1]
+        for part in range(share_ref.shape[0]):
+            share_ref[part] = partial_ref[part * rows : (part + 1) * rows, :].astype(BF16)
+
+
+def attention(start, queries, keys, values, memory, weight, grad, parts):
     tokens, width = queries.shape
     full = weight.shape[1]
-    pooled = memory.shape[2]
-    extent = MEM * (-(-pooled // 8) * 8) + tokens
+    pitch = memory.shape[2]
+    extent = MEM * pitch + tokens
     columns = pl.BlockSpec((tokens, LANES), lambda i: (0, i))
-    memory_block = pl.BlockSpec((MEM, 2, pooled, LANES), lambda i: (0, 0, 0, i))
+    memory_block = pl.BlockSpec((MEM, 2, pitch, LANES), lambda i: (0, 0, 0, i))
     return pl.pallas_call(
         attention_kernel,
         grid=(width // LANES,),
@@ -123,58 +132,286 @@
             pl.BlockSpec((tokens, full), lambda i: (0, 0)),
         ],
         out_specs=[
-            pl.BlockSpec((tokens, full), lambda i: (0, 0)),
+            pl.BlockSpec((parts, tokens // parts, full), lambda i: (0, 0, 0)),
             columns,
             pl.BlockSpec((2, tokens, LANES), lambda i: (0, 0, i)),
             memory_block,
         ],
         out_shape=[
-            jax.ShapeDtypeStruct((tokens, full), F32),
+            jax.ShapeDtypeStruct((parts, tokens // parts, full), BF16),
             jax.ShapeDtypeStruct((tokens, width), BF16),
             jax.ShapeDtypeStruct((2, tokens, width), F32),
-            jax.ShapeDtypeStruct((MEM, 2, pooled, width), BF16),
-        ],
-        scratch_shapes=[pltpu.VMEM((extent, LANES), F32)] * 3,
+            jax.ShapeDtypeStruct((MEM, 2, pitch, width), BF16),
+        ],
+        scratch_shapes=[pltpu.VMEM((extent, LANES), F32)] * 3 + [pltpu.VMEM((tokens, full), F32)],
         compiler_params=pltpu.CompilerParams(dimension_semantics=("arbitrary",)),
         name="attention",
-    )(flags, queries, keys, values, memory, weight, grad)
-
-
-def passed_along(block, axis, distance):
-    devices = range(lax.axis_size(axis))
-    route = [(i - distance, i) for i in devices if i - distance in devices]
-    return lax.ppermute(block, axis, route)
+    )(start, queries, keys, values, memory, weight, grad)
+
+
+def remote(source, target, send, receive, device):
+    return pltpu.make_async_remote_copy(
+        src_ref=source,
+        dst_ref=target,
+        send_sem=send,
+        recv_sem=receive,
+        device_id=device,
+        device_id_type=pl.DeviceIdType.MESH,
+    )
+
+
+def place(count):
+    me = lax.axis_index("tm")
+    core = lax.rem(me, 2)
+    side = lax.rem(me // 2, 2)
+    sibling = {"tm": me + 1 - 2 * core}
+    across = {"tm": me + 2 - 4 * side}
+    later = {"tm": lax.rem(me + GROUP, count)}
+    earlier = {"tm": lax.rem(me + count - GROUP, count)}
+    return me, core, side, sibling, across, later, earlier, me + GROUP < count, me >= GROUP
+
+
+def greet(neighbours):
+    barrier = pltpu.get_barrier_semaphore()
+    for device in neighbours:
+        pl.semaphore_signal(
+            barrier, inc=1, device_id=device, device_id_type=pl.DeviceIdType.MESH
+        )
+    pl.semaphore_wait(barrier, len(neighbours))
+
+
+def gather_kernel(count, start, k_ref, v_ref, out_ref, buf, send, receive, stored):
+    me, core, side, sibling, across, later, earlier, has_later, has_earlier = place(count)
+    tokens, width = k_ref.shape
+    pooled = tokens // POOL
+    pitch = out_ref.shape[2]
+    row = lax.broadcasted_iota(jnp.int32, (pitch, tokens), 0)
+    token = lax.broadcasted_iota(jnp.int32, (pitch, tokens), 1)
+    inside = (token >= row * POOL) & (token < row * POOL + POOL)
+    mixing = jnp.where(inside, 1.0 / POOL, 0.0).astype(BF16)
+    line = lax.broadcasted_iota(jnp.int32, (pitch, width), 0)
+    keep = jnp.full((pitch, width), 1 - start[0], jnp.int32).astype(F32)
+    for which, ref in enumerate((k_ref, v_ref)):
+        mean = jnp.dot(mixing, ref[...], preferred_element_type=F32)
+        mean = jnp.where(line == pooled, keep, jnp.where(line == pooled + 1, 1.0, mean))
+        buf[0, which] = mean.astype(BF16)
+
+    @pl.when(jnp.logical_not(has_earlier))
+    def _():
+        for slot in (4, 8):
+            buf[slot] = jnp.zeros(buf.shape[1:], BF16)
+
+    greet([sibling, across, later, earlier])
+
+    def move(source, target, which, number, device):
+        return remote(
+            buf.at[source, which], buf.at[target, which],
+            send.at[number, which], receive.at[target, which], device,
+        )
+
+    def arrive(slot, which):
+        move(slot, slot, which, 0, sibling).wait_recv()
+
+    def store(slot, which):
+        pltpu.make_async_copy(
+            buf.at[slot, which], out_ref.at[slot - 1, which], stored.at[slot - 1, which]
+        ).start()
+
+    for which in range(2):
+        pl.when(has_later)(lambda: move(0, 4, which, 0, later).start())
+        pl.when(side == 0)(lambda: move(0, 2, which, 2, across).start())
+        pl.when(core == 0)(lambda: move(0, 1, which, 4, sibling).start())
+    for which in range(2):
+        pl.when(has_earlier)(lambda: arrive(4, which))
+        pl.when(has_later)(lambda: move(4, 8, which, 1, later).start())
+        pl.when(side == 0)(lambda: move(4, 6, which, 3, across).start())
+        pl.when(side == 1)(lambda: move(4, 2, which, 2, across).start())
+        pl.when(core == 0)(lambda: move(4, 5, which, 5, sibling).start())
+        pl.when(core == 1)(lambda: move(4, 3, which, 4, sibling).start())
+        store(4, which)
+    for which in range(2):
+        arrive(2, which)
+        pl.when(core == 0)(lambda: move(2, 3, which, 6, sibling).start())
+        pl.when(core == 1)(lambda: move(2, 1, which, 6, sibling).start())
+        store(2, which)
+    for which in range(2):
+        pl.when(has_earlier)(lambda: arrive(8, which))
+        pl.when(side == 1)(lambda: move(8, 6, which, 3, across).start())
+        pl.when(core == 1)(lambda: move(8, 7, which, 5, sibling).start())
+        store(8, which)
+    for which in range(2):
+        arrive(6, which)
+        pl.when(core == 0)(lambda: move(6, 7, which, 7, sibling).start())
+        pl.when(core == 1)(lambda: move(6, 5, which, 7, sibling).start())
+        store(6, which)
+    for slot in (1, 3, 5, 7):
+        for which in range(2):
+            arrive(slot, which)
+            store(slot, which)
+    for which in range(2):
+        for number in (0, 1):
+            pl.when(has_later)(lambda: move(0, 4, which, number, later).wait_send())
+        for number in range(2, 8):
+            move(0, 2, which, number, across).wait_send()
+        for slot in range(1, MEM + 1):
+            pltpu.make_async_copy(
+                buf.at[slot, which], out_ref.at[slot - 1, which], stored.at[slot - 1, which]
+            ).wait()
+
+
+def gather(start, keys, values, count):
+    tokens, width = keys.shape
+    pitch = -(-(tokens // POOL + 2) // 8) * 8
+    whole = pl.BlockSpec(memory_space=pltpu.VMEM)
+    return pl.pallas_call(
+        functools.partial(gather_kernel, count),
+        in_specs=[pl.BlockSpec(memory_space=pltpu.SMEM), whole, whole],
+        out_specs=pl.BlockSpec(memory_space=pl.ANY),
+        out_shape=jax.ShapeDtypeStruct((MEM, 2, pitch, width), BF16),
+        scratch_shapes=[
+            pltpu.VMEM((MEM + 1, 2, pitch, width), BF16),
+            pltpu.SemaphoreType.DMA((8, 2)),
+            pltpu.SemaphoreType.DMA((MEM + 1, 2)),
+            pltpu.SemaphoreType.DMA((MEM, 2)),
+        ],
+        compiler_params=pltpu.CompilerParams(collective_id=1, has_side_effects=True),
+        name="gather",
+    )(start, keys, values)
+
+
+def giving_kernel(
+    count, parts, grads, own_ref, share_ref, projected_ref, dk_ref, dv_ref,
+    landed, sums, shares, send, receive, share_send, share_receive,
+):
+    me, core, side, sibling, across, later, earlier, has_later, has_earlier = place(count)
+    head = lax.axis_index("head")
+    tokens = own_ref.shape[1]
+    pitch = grads.shape[2]
+
+    @pl.when(jnp.logical_not(has_later))
+    def _():
+        for number in (6, 7):
+            landed[number] = jnp.zeros(landed.shape[1:], BF16)
+
+    peers = [{"head": lax.rem(head + k, parts)} for k in range(1, parts)]
+    greet([sibling, across, later, earlier] + peers)
+
+    def move(source, number, which, device):
+        return remote(
+            source, landed.at[number, which],
+            send.at[number, which], receive.at[number, which], device,
+        )
+
+    def slot(index, which):
+        return grads.at[index - 1, which]
+
+    for which in range(2):
+        for number, bottom, step in ((3, 5, 2), (1, 7, -2), (2, 1, 2), (0, 3, -2)):
+            move(slot(bottom + step * core, which), number, which, sibling).start()
+    exchanges = []
+    for k, peer in enumerate(peers):
+        copy = remote(
+            share_ref.at[lax.rem(head + k + 1, parts)], shares.at[k],
+            share_send.at[k], share_receive.at[k], peer,
+        )
+        copy.start()
+        exchanges.append(copy)
+
+    def arrive(number, which):
+        move(slot(1, which), number, which, sibling).wait_recv()
+        return landed[number, which].astype(F32)
+
+    is_core = core.astype(F32)
+    is_side = side.astype(F32)
+    for which in range(2):
+        sums[1, which] = (grads[5, which].astype(F32) + arrive(3, which)).astype(BF16)
+        move(sums.at[1, which], 5, which, across).start()
+    for which in range(2):
+        from_core = arrive(1, which)
+        sums[0, which] = (grads[1, which].astype(F32) + arrive(2, which)).astype(BF16)
+        move(sums.at[0, which], 4, which, across).start()
+    for which in range(2):
+        total = grads[7, which].astype(F32) + is_core * landed[1, which].astype(F32)
+        total = total + is_side * arrive(5, which)
+        sums[3, which] = total.astype(BF16)
+        pl.when(has_earlier)(lambda: move(sums.at[3, which], 7, which, earlier).start())
+    for which in range(2):
+        total = grads[3, which].astype(F32) + (1 - is_core) * landed[1, which].astype(F32)
+        total = total + is_core * arrive(0, which)
+        total = total + (1 - is_side) * landed[5, which].astype(F32)
+        total = total + is_side * arrive(4, which)
+        pl.when(has_later)(
+            lambda: move(slot(1, which), 7, which, sibling).wait_recv()
+        )
+        total = total + landed[7, which].astype(F32)
+        sums[2, which] = total.astype(BF16)
+        pl.when(has_earlier)(lambda: move(sums.at[2, which], 6, which, earlier).start())
+
+    for copy in exchanges:
+        copy.wait()
+    projected = share_ref[head].astype(F32)
+    for k in range(parts - 1):
+        projected = projected + shares[k].astype(F32)
+    projected_ref[...] = projected.astype(BF16)
+
+    token = lax.broadcasted_iota(jnp.int32, (tokens, pitch), 0)
+    row = lax.broadcasted_iota(jnp.int32, (tokens, pitch), 1)
+    inside = (token >= row * POOL) & (token < row * POOL + POOL)
+    spread = jnp.where(inside, 1.0 / POOL, 0.0).astype(BF16)
+    for which, ref in enumerate((dk_ref, dv_ref)):
+        pl.when(has_later)(
+            lambda: move(slot(1, which), 6, which, sibling).wait_recv()
+        )
+        total = (1 - is_core) * landed[0, which].astype(F32) + landed[6, which].astype(F32)
+        total = total + (1 - is_side) * landed[4, which].astype(F32)
+        shared = jnp.dot(spread, total.astype(BF16), preferred_element_type=F32)
+        ref[...] = (own_ref[which] + shared).astype(BF16)
+    for which in range(2):
+        for number in range(6):
+            move(slot(1, which), number, which, sibling).wait_send()
+        for number in (6, 7):
+            pl.when(has_earlier)(
+                lambda: move(slot(1, which), number, which, sibling).wait_send()
+            )
+
+
+def give_back(grads, own, share, count):
+    _, tokens, width = own.shape
+    parts, rows, full = share.shape
+    pitch = grads.shape[2]
+    whole = pl.BlockSpec(memory_space=pltpu.VMEM)
+    return pl.pallas_call(
+        functools.partial(giving_kernel, count, parts),
+        in_specs=[whole] * 3,
+        out_specs=[whole] * 3,
+        out_shape=[
+            jax.ShapeDtypeStruct((rows, full), BF16),
+            jax.ShapeDtypeStruct((tokens, width), BF16),
+            jax.ShapeDtypeStruct((tokens, width), BF16),
+        ],
+        scratch_shapes=[
+            pltpu.VMEM((8, 2, pitch, width), BF16),
+            pltpu.VMEM((4, 2, pitch, width), BF16),
+            pltpu.VMEM((parts - 1, rows, full), BF16),
+            pltpu.SemaphoreType.DMA((8, 2)),
+            pltpu.SemaphoreType.DMA((8, 2)),
+            pltpu.SemaphoreType.DMA((parts - 1,)),
+            pltpu.SemaphoreType.DMA((parts - 1,)),
+        ],
+        compiler_params=pltpu.CompilerParams(collective_id=2, has_side_effects=True),
+        name="give_back",
+    )(grads, own, share)
 
 
 def local(queries, key_tokens, value_tokens, out_weight, out_grad, clip_starts):
-    token_count, local_width = queries.shape[1:]
-    pooled_count = token_count // POOL
-    pooled_own = (
-        jnp.stack([key_tokens[0], value_tokens[0]])
-        .astype(F32)
-        .reshape(2, pooled_count, POOL, local_width)
-        .mean(axis=2)
-        .astype(BF16)
+    count = lax.axis_size("tm")
+    memory = gather(clip_starts, key_tokens[0], value_tokens[0], count)
+    share, dq, own, memory_grads = attention(
+        clip_starts, queries[0], key_tokens[0], value_tokens[0], memory, out_weight, out_grad[0],
+        lax.axis_size("head"),
     )
-    starts = lax.all_gather(clip_starts.astype(F32), "tm", tiled=True)
-    mine = lax.axis_index("tm")
-    running = 1 - clip_starts[0].astype(F32)
-    flags = []
-    for distance in range(1, MEM + 1):
-        earlier = mine - distance
-        flags.append(jnp.where(earlier >= 0, running, 0.0))
-        running = running * (1 - starts[jnp.maximum(earlier, 0)])
-    memory = jnp.stack([passed_along(pooled_own, "tm", d) for d in range(1, MEM + 1)])
-    partial, dq, own, memory_grads = attention(
-        jnp.stack(flags).astype(jnp.int32),
-        queries[0], key_tokens[0], value_tokens[0], memory, out_weight, out_grad[0],
-    )
-    projected = lax.psum_scatter(partial, "head", scatter_dimension=0, tiled=True).astype(BF16)
-    returned = jnp.zeros((2, pooled_count, local_width), F32)
-    for distance in range(1, MEM + 1):
-        returned = returned + passed_along(memory_grads[distance - 1], "tm", -distance).astype(F32)
-    both = (own + jnp.repeat(returned, POOL, axis=1) / POOL).astype(BF16)
-    return (projected[None], dq[None], both[:1], both[1:])
+    projected, dk, dv = give_back(memory_grads, own, share, count)
+    return (projected[None], dq[None], dk[None], dv[None])
 
 
 def solution(mesh):

time: 182 us -> 78.8 us (0.43)
  the two profiles are of different devices: /device:TPU:11 before, /device:TPU:0 now
where the time goes in v2:
time: 78.8 us; the launch traced here: 78.6 us
  Pallas kernels  72.9 us (93%)
  local copies, waits for them, and re-layouts  4.35 us (6%)
  between operations  1.3 us (2%)
    pallas_call x1, Pallas kernels, attention(): pl.pallas_call(attention_kernel, grid=(width // LANES,), in_specs=[pl.Blo...  28 us
    pallas_call x1, Pallas kernels, give_back(): pl.pallas_call(functools.partial(giving_kernel, count, parts), in_specs=[...  25 us
    pallas_call x1, Pallas kernels, gather(): pl.pallas_call(functools.partial(gather_kernel, count), in_specs=[pl.Bloc...  19.9 us
    unnamed x5, local copies, waits for them, and re-layouts  4.35 us

profile of v2, /device:TPU:0, one launch (start us, length us, event | category | flops | bytes accessed | tf_op | source)
XLA Modules:
  0.0 78.6 jit_solution(15510387715725940092)
XLA Ops:
  1.3 19.9 %gather.1.mem_ref = bf16[8,2,104,512]{3,2,1,0:T(8,128)(2,1)} custom-call(s32[1]{0:T(128)S(6)} %copy.13.start, bf16[392,512]{1,0:T(8,128)(2,1)} %bitcast.8, bf16[392,512]{1,0:T(8,128)(2,1)} %bitcast.10), custom_call_target="tpu_custom_call" | custom-call | tf_op jit(solution)/shard_map/gather/pallas_call | solution.py:266
  21.2 28.0 %attention.1 = (bf16[2,196,1024]{2,1,0:T(8,128)(2,1)}, bf16[392,512]{1,0:T(8,128)(2,1)}, f32[2,392,512]{2,1,0:T(8,128)}, bf16[8,2,104,512]{3,2,1,0:T(8,128)(2,1)}) custom-call(s32[1]{0:T(128)S(6)} %copy.13.start, bf16[392,512]{1,0:T(8,128)(2,1)} %bitcast.14, bf16[392,512]{1,0:T(8,128)(2,1)} %bitcast.9, bf16[392,512]{1,0:T(8,128)(2,1)} %bitcast.11, ...), custom_call_target="tpu_custom_call" | custom-call | tf_op jit(solution)/shard_map/attention/pallas_call | solution.py:122
  49.2 25.0 %give_back.1 = (bf16[196,1024]{1,0:T(8,128)(2,1)}, bf16[392,512]{1,0:T(8,128)(2,1)}, bf16[392,512]{1,0:T(8,128)(2,1)}) custom-call(bf16[8,2,104,512]{3,2,1,0:T(8,128)(2,1)} %get-tuple-element.11.grads, f32[2,392,512]{2,1,0:T(8,128)} %get-tuple-element.12.own_ref, bf16[2,196,1024]{2,1,0:T(8,128)(2,1)} %get-tuple-element.13.share_ref), custom_call_target="tpu_custom_call" | custom-call | tf_op jit(solution)/shard_map/give_back/pallas_call | solution.py:383
  74.2 0.0 copy-start
  74.2 1.8 %copy.14 = bf16[1,196,1024]{2,1,0:T(8,128)(2,1)} copy(bf16[1,196,1024]{2,1,0:T(8,128)(2,1)} %bitcast.13) | data formatting | bytes 802816
  76.1 1.8 %copy.15 = bf16[1,392,512]{2,1,0:T(8,128)(2,1)} copy(bf16[1,392,512]{2,1,0:T(8,128)(2,1)} %bitcast.16) | data formatting | bytes 802816
  77.8 0.0 copy-done
  77.8 0.7 copy.16
Async XLA Ops:
  74.2 3.6 %copy-start = (bf16[392,512]{1,0:T(8,128)(2,1)S(1)}, bf16[392,512]{1,0:T(8,128)(2,1)}, u32[]{:S(2)}) copy-start(bf16[392,512]{1,0:T(8,128)(2,1)} %get-tuple-element.17) | copy-start | bytes 1204228

commit v3 on v2

--- a/solution.py
+++ b/solution.py
@@ -280,13 +280,11 @@
 
 
 def giving_kernel(
-    count, parts, grads, own_ref, share_ref, projected_ref, dk_ref, dv_ref,
+    count, parts, grads, share_ref, projected_ref, returned_ref,
     landed, sums, shares, send, receive, share_send, share_receive,
 ):
     me, core, side, sibling, across, later, earlier, has_later, has_earlier = place(count)
     head = lax.axis_index("head")
-    tokens = own_ref.shape[1]
-    pitch = grads.shape[2]
 
     @pl.when(jnp.logical_not(has_later))
     def _():
@@ -354,18 +352,13 @@
         projected = projected + shares[k].astype(F32)
     projected_ref[...] = projected.astype(BF16)
 
-    token = lax.broadcasted_iota(jnp.int32, (tokens, pitch), 0)
-    row = lax.broadcasted_iota(jnp.int32, (tokens, pitch), 1)
-    inside = (token >= row * POOL) & (token < row * POOL + POOL)
-    spread = jnp.where(inside, 1.0 / POOL, 0.0).astype(BF16)
-    for which, ref in enumerate((dk_ref, dv_ref)):
+    for which in range(2):
         pl.when(has_later)(
             lambda: move(slot(1, which), 6, which, sibling).wait_recv()
         )
         total = (1 - is_core) * landed[0, which].astype(F32) + landed[6, which].astype(F32)
         total = total + (1 - is_side) * landed[4, which].astype(F32)
-        shared = jnp.dot(spread, total.astype(BF16), preferred_element_type=F32)
-        ref[...] = (own_ref[which] + shared).astype(BF16)
+        returned_ref[which] = total.astype(BF16)
     for which in range(2):
         for number in range(6):
             move(slot(1, which), number, which, sibling).wait_send()
@@ -375,19 +368,17 @@
             )
 
 
-def give_back(grads, own, share, count):
-    _, tokens, width = own.shape
+def give_back(grads, share, count):
     parts, rows, full = share.shape
-    pitch = grads.shape[2]
+    pitch, width = grads.shape[2:]
     whole = pl.BlockSpec(memory_space=pltpu.VMEM)
     return pl.pallas_call(
         functools.partial(giving_kernel, count, parts),
-        in_specs=[whole] * 3,
-        out_specs=[whole] * 3,
+        in_specs=[whole] * 2,
+        out_specs=[whole] * 2,
         out_shape=[
             jax.ShapeDtypeStruct((rows, full), BF16),
-            jax.ShapeDtypeStruct((tokens, width), BF16),
-            jax.ShapeDtypeStruct((tokens, width), BF16),
+            jax.ShapeDtypeStruct((2, pitch, width), BF16),
         ],
         scratch_shapes=[
             pltpu.VMEM((8, 2, pitch, width), BF16),
@@ -400,7 +391,46 @@
         ],
         compiler_params=pltpu.CompilerParams(collective_id=2, has_side_effects=True),
         name="give_back",
-    )(grads, own, share)
+    )(grads, share)
+
+
+def finish_kernel(own_ref, returned_ref, share_ref, projected_ref, dk_ref, dv_ref):
+    tokens = own_ref.shape[1]
+    pitch = returned_ref.shape[1]
+    token = lax.broadcasted_iota(jnp.int32, (tokens, pitch), 0)
+    row = lax.broadcasted_iota(jnp.int32, (tokens, pitch), 1)
+    inside = (token >= row * POOL) & (token < row * POOL + POOL)
+    spread = jnp.where(inside, 1.0 / POOL, 0.0).astype(BF16)
+    for which, ref in enumerate((dk_ref, dv_ref)):
+        shared = jnp.dot(spread, returned_ref[which], preferred_element_type=F32)
+        ref[...] = (own_ref[which] + shared).astype(BF16)
+    projected_ref[...] = share_ref[...]
+
+
+def finish(own, returned, share):
+    _, tokens, width = own.shape
+    pitch = returned.shape[1]
+    rows, full = share.shape
+    steps = width // LANES
+    columns = pl.BlockSpec((tokens, LANES), lambda i: (0, i))
+    shares = pl.BlockSpec((rows, full // steps), lambda i: (0, i))
+    return pl.pallas_call(
+        finish_kernel,
+        grid=(steps,),
+        in_specs=[
+            pl.BlockSpec((2, tokens, LANES), lambda i: (0, 0, i)),
+            pl.BlockSpec((2, pitch, LANES), lambda i: (0, 0, i)),
+            shares,
+        ],
+        out_specs=[shares, columns, columns],
+        out_shape=[
+            jax.ShapeDtypeStruct((rows, full), BF16),
+            jax.ShapeDtypeStruct((tokens, width), BF16),
+            jax.ShapeDtypeStruct((tokens, width), BF16),
+        ],
+        compiler_params=pltpu.CompilerParams(dimension_semantics=("arbitrary",)),
+        name="finish",
+    )(own, returned, share)
 
 
 def local(queries, key_tokens, value_tokens, out_weight, out_grad, clip_starts):
@@ -410,7 +440,8 @@
         clip_starts, queries[0], key_tokens[0], value_tokens[0], memory, out_weight, out_grad[0],
         lax.axis_size("head"),
     )
-    projected, dk, dv = give_back(memory_grads, own, share, count)
+    share, returned = give_back(memory_grads, share, count)
+    projected, dk, dv = finish(own, returned, share)
     return (projected[None], dq[None], dk[None], dv[None])
 
 

time: 78.8 us -> 77.6 us (0.985)
  local copies, waits for them, and re-layouts: 4.35 us -> 0 us
  Pallas kernels: 72.9 us -> 76.1 us
    unnamed x5 -> x0, local copies, waits for them, and re-layouts: 4.35 us -> none
    pallas_call x0 -> x1, Pallas kernels: none -> 4.02 us  [finish(): pl.pallas_call(finish_kernel, grid=(steps,), in_specs=[pl.BlockSpec((2, t...]
    pallas_call x1, Pallas kernels: 25 us -> 24.1 us  [give_back(): pl.pallas_call(functools.partial(giving_kernel, count, parts), in_specs=[...]
where the time goes in v3:
time: 77.6 us; the launch traced here: 77.4 us
  Pallas kernels  76.1 us (98%)
  between operations  1.29 us (2%)
    pallas_call x1, Pallas kernels, attention(): pl.pallas_call(attention_kernel, grid=(width // LANES,), in_specs=[pl.Blo...  28 us
    pallas_call x1, Pallas kernels, give_back(): pl.pallas_call(functools.partial(giving_kernel, count, parts), in_specs=[...  24.1 us
    pallas_call x1, Pallas kernels, gather(): pl.pallas_call(functools.partial(gather_kernel, count), in_specs=[pl.Bloc...  19.9 us
    pallas_call x1, Pallas kernels, finish(): pl.pallas_call(finish_kernel, grid=(steps,), in_specs=[pl.BlockSpec((2, t...  4.02 us

profile of v3, /device:TPU:0, one launch (start us, length us, event | category | flops | bytes accessed | tf_op | source)
XLA Modules:
  0.0 77.4 jit_solution(3200119777707729927)
XLA Ops:
  1.3 19.9 %gather.1.mem_ref = bf16[8,2,104,512]{3,2,1,0:T(8,128)(2,1)} custom-call(s32[1]{0:T(128)S(6)} %copy.10.start, bf16[392,512]{1,0:T(8,128)(2,1)} %bitcast.8, bf16[392,512]{1,0:T(8,128)(2,1)} %bitcast.10), custom_call_target="tpu_custom_call" | custom-call | tf_op jit(solution)/shard_map/gather/pallas_call | solution.py:266
  21.2 28.0 %attention.1 = (bf16[2,196,1024]{2,1,0:T(8,128)(2,1)}, bf16[392,512]{1,0:T(8,128)(2,1)}, f32[2,392,512]{2,1,0:T(8,128)}, bf16[8,2,104,512]{3,2,1,0:T(8,128)(2,1)}) custom-call(s32[1]{0:T(128)S(6)} %copy.10.start, bf16[392,512]{1,0:T(8,128)(2,1)} %bitcast.13, bf16[392,512]{1,0:T(8,128)(2,1)} %bitcast.9, bf16[392,512]{1,0:T(8,128)(2,1)} %bitcast.11, ...), custom_call_target="tpu_custom_call" | custom-call | tf_op jit(solution)/shard_map/attention/pallas_call | solution.py:122
  49.2 24.1 %give_back.1 = (bf16[196,1024]{1,0:T(8,128)(2,1)}, bf16[2,104,512]{2,1,0:T(8,128)(2,1)}) custom-call(bf16[8,2,104,512]{3,2,1,0:T(8,128)(2,1)} %get-tuple-element.14.grads, bf16[2,196,1024]{2,1,0:T(8,128)(2,1)} %get-tuple-element.15.share_ref), custom_call_target="tpu_custom_call" | custom-call | tf_op jit(solution)/shard_map/give_back/pallas_call | solution.py:375
  73.3 4.0 %finish.1 = (bf16[196,1024]{1,0:T(8,128)(2,1)}, bf16[392,512]{1,0:T(8,128)(2,1)}, bf16[392,512]{1,0:T(8,128)(2,1)}) custom-call(f32[2,392,512]{2,1,0:T(8,128)} %get-tuple-element.13.own_ref, bf16[2,104,512]{2,1,0:T(8,128)(2,1)} %get-tuple-element.16.returned_ref, bf16[196,1024]{1,0:T(8,128)(2,1)} %get-tuple-element.17.share_ref), custom_call_target="tpu_custom_call" | custom-call | tf_op jit(solution)/shard_map/finish/pallas_call | solution.py:417
